TPU v7x, 32 devices: a whole 2x2x4 slice. The times are simulated.
32 devices in a mesh: dp: 8 (over z, x), tensor: 4 (over y, core).
Axes of the slice: x: 2, y: 2, z: 4, core: 2. Of those that a mesh axis runs over, the one named last changes fastest.
Arguments:
- features: bfloat16 [3072, 8192], P('dp', 'tensor'), may hold values from -6 to 6
- key_value_weight: bfloat16 [8192, 2048], P('tensor'), may hold values from -0.0625 to 0.0625
- adapter_down_weight: bfloat16 [32, 64, 8192], P('dp', None, 'tensor'), may hold values from -0.0625 to 0.0625
- adapter_up_weight: bfloat16 [32, 64, 2048], P('dp', None, 'tensor'), may hold values from -0.75 to 0.75
- token_adapter_index: int32 [3072], P('dp'), may hold values from 0 to 31, as said below
- adapter_position: int32 [32], replicated, may hold values from 0 to 31, as said below
- output_gradient: bfloat16 [3072, 2048], P('dp', 'tensor'), may hold values from -6 to 6
Outputs:
- key_value_output: bfloat16 [3072, 2048], P('dp', 'tensor')
- feature_gradient: bfloat16 [3072, 8192], P('dp', 'tensor')
- down_gradient: float32 [32, 64, 8192], P('dp', None, 'tensor')
- up_gradient: float32 [32, 64, 2048], P('dp', None, 'tensor')
Inputs may be any that keep to these rules, and one draw needn't show every extreme that they name: `token_adapter_index`: within each aligned block of 384 tokens (those of one index of dp) the ids do not fall. Call slot // 4 the storing index of an adapter; in each block at most 144 tokens have adapters of one storing index. In every draw one storing index, the same for all blocks, gets exactly 144 tokens from every block, and in every block another storing index, which varies from block to block, gets exactly 144 tokens as well. A permutation: adapter a is stored at slot adapter_position[a].
All inputs are finite; a program needn't handle non-finite values.
Results may differ from a plain program's by a relative error of at most 0.0054.
Values may be sent and summed in bfloat16 or wider, within the bound.
A program may use at most 64 MiB of HBM per device.

v0:
```python
import jax
import jax.numpy as jnp
from jax import lax
from jax.sharding import PartitionSpec as P

adapter_scale = 2.0


def contract_trailing(left, right):
    return lax.dot_general(
        left, right, (((1,), (1,)), ((), ())), preferred_element_type=jnp.float32
    )


def contract_leading(left, right):
    return lax.dot_general(
        left, right, (((0,), (0,)), ((), ())), preferred_element_type=jnp.float32
    )


def body(
    features,
    key_value_weight,
    adapter_down_weight,
    adapter_up_weight,
    token_adapter_index,
    adapter_position,
    output_gradient,
):
    token_groups = lax.axis_size("dp")
    tok_rows, width_local = features.shape
    output_local = output_gradient.shape[1]
    adapter_local_count, rank_axis_size, unused_value = adapter_down_weight.shape
    row_capacity = 3 * tok_rows // token_groups
    holding_rows = token_groups * row_capacity
    adapter_ids = jnp.arange(adapter_position.shape[0], dtype=jnp.int32)
    matches = token_adapter_index[:, None] == adapter_ids[None, :]
    slot_tok = jnp.sum(jnp.where(matches, adapter_position[None, :], 0), axis=1)
    owner_of = slot_tok // adapter_local_count
    local_id = slot_tok % adapter_local_count
    owner_hits = (owner_of[:, None] == jnp.arange(token_groups, dtype=jnp.int32)[None, :]).astype(
        jnp.int32
    )
    rank_in = jnp.sum((jnp.cumsum(owner_hits, axis=0) - 1) * owner_hits, axis=1)
    target_slot = owner_of * row_capacity + rank_in

    def to_buffer(source):
        filled = (
            jnp.zeros((holding_rows, source.shape[1]), source.dtype).at[target_slot].set(source)
        )
        return filled.reshape(token_groups, row_capacity, source.shape[1])

    id_buffer = (
        jnp.full((holding_rows,), -1.0, jnp.bfloat16)
        .at[target_slot]
        .set(local_id.astype(jnp.bfloat16))
    )
    id_buffer = id_buffer.reshape(token_groups, row_capacity)
    lane_ids = (
        jnp.arange(adapter_local_count * rank_axis_size, dtype=jnp.int32) // rank_axis_size
    ).astype(jnp.bfloat16)
    down_matrix = adapter_down_weight.reshape(adapter_local_count * rank_axis_size, width_local)
    up_matrix = adapter_up_weight.reshape(adapter_local_count * rank_axis_size, output_local)

    def compact_rows(values, slot_selector):
        return jnp.sum(
            (values * slot_selector).reshape(holding_rows, adapter_local_count, rank_axis_size),
            axis=1,
        )

    def expand(values, slot_selector):
        return (
            jnp.tile(values, (1, adapter_local_count)).astype(jnp.float32) * slot_selector
        ).astype(jnp.bfloat16)

    columns = key_value_weight
    gradient_frozen = contract_trailing(
        lax.all_gather(output_gradient, "tensor", axis=1, tiled=True), columns
    )
    rows_recv, ids_recv = (
        lax.all_to_all(to_buffer(features), "dp", split_axis=0, concat_axis=0, tiled=True),
        lax.all_to_all(id_buffer, "dp", split_axis=0, concat_axis=0, tiled=True),
    )
    rows_in = rows_recv.reshape(holding_rows, width_local)
    slot_selector = (ids_recv.reshape(holding_rows)[:, None] == lane_ids[None, :]).astype(
        jnp.float32
    )
    down_part = compact_rows(contract_trailing(rows_in, down_matrix), slot_selector)
    down_total = lax.psum(down_part, "tensor")
    down_gathered = expand(down_total.astype(jnp.bfloat16), slot_selector)
    adapter_row_block = (
        adapter_scale * jnp.dot(down_gathered, up_matrix, preferred_element_type=jnp.float32)
    ).astype(jnp.bfloat16)
    adapter_backward = lax.all_to_all(
        adapter_row_block.reshape(token_groups, row_capacity, output_local),
        "dp",
        split_axis=0,
        concat_axis=0,
        tiled=True,
    )
    grads_recv = lax.all_to_all(
        to_buffer(output_gradient), "dp", split_axis=0, concat_axis=0, tiled=True
    )
    incoming_gradients = grads_recv.reshape(holding_rows, output_local)
    up_partial = compact_rows(
        adapter_scale * contract_trailing(incoming_gradients, up_matrix), slot_selector
    )
    up_combined = lax.psum(up_partial, "tensor")
    up_wide = expand(up_combined.astype(jnp.bfloat16), slot_selector)
    input_row_block = jnp.dot(up_wide, down_matrix, preferred_element_type=jnp.float32).astype(
        jnp.bfloat16
    )
    input_back = lax.all_to_all(
        input_row_block.reshape(token_groups, row_capacity, width_local),
        "dp",
        split_axis=0,
        concat_axis=0,
        tiled=True,
    )
    down_gradient = contract_leading(up_wide, rows_in).reshape(
        adapter_local_count, rank_axis_size, width_local
    )
    up_gradient = (adapter_scale * contract_leading(down_gathered, incoming_gradients)).reshape(
        adapter_local_count, rank_axis_size, output_local
    )
    adapter_token_rows = adapter_backward.reshape(holding_rows, output_local)[target_slot]
    input_tok = input_back.reshape(holding_rows, width_local)[target_slot]
    columns = key_value_weight
    key_value_frozen = lax.psum_scatter(
        contract_leading(columns, features.T), "tensor", scatter_dimension=0, tiled=True
    ).T
    key_value_output = (key_value_frozen + adapter_token_rows.astype(jnp.float32)).astype(
        jnp.bfloat16
    )
    feature_gradient = (gradient_frozen + input_tok.astype(jnp.float32)).astype(jnp.bfloat16)
    return (key_value_output, feature_gradient, down_gradient, up_gradient)


def solution(mesh):
    placed = (
        P("dp", "tensor"),
        P("tensor", None),
        P("dp", None, "tensor"),
        P("dp", None, "tensor"),
        P("dp"),
        P(),
        P("dp", "tensor"),
    )
    return jax.shard_map(
        body,
        mesh=mesh,
        in_specs=placed,
        out_specs=(
            P("dp", "tensor"),
            P("dp", "tensor"),
            P("dp", None, "tensor"),
            P("dp", None, "tensor"),
        ),
        check_vma=False,
    )
```

profile of v0, /device:TPU:11, one launch (start us, length us, event | category | flops | bytes accessed | tf_op | source)
XLA Modules:
  0.0 350.5 jit_solution(9046061355832921624)
XLA Ops:
  9.4 3.0 scatter_custom_fusion
  13.0 5.7 %all-to-all-start = ((bf16[8,1,144]{2,1,0:T(2,128)(2,1)}), bf16[8,1,144]{2,1,0:T(2,128)(2,1)S(1)}, u32[]{:S(2)}, u32[]{:S(2)}) async-start(bf16[8,1,144]{2,1,0:T(2,128)(2,1)} %all_to_all.24), calls=%async_computation.1 | async-start | bytes 16384 | tf_op jit(solution)/shard_map/all_to_all | solution.py:82
  18.7 3.6 %scatter_custom_fusion.2 = bf16[1152,512]{1,0:T(8,128)(2,1)} fusion(s32[384]{0:T(512)S(1)} %fusion.27, bf16[384,512]{1,0:T(8,128)(2,1)} %param.13, bf16[]{:T(256)} %constant.71.clone.1), kind=kCustom, calls=%fused_computation.25 | custom fusion | bytes 1180160 | tf_op jit(solution)/shard_map/scatter | solution.py:49
  22.2 5.4 %all-to-all-start.3 = ((bf16[8,144,512]{2,1,0:T(8,128)(2,1)}), bf16[8,144,512]{2,1,0:T(8,128)(2,1)S(1)}, u32[]{:S(2)}, u32[]{:S(2)}) async-start(bf16[8,144,512]{2,1,0:T(8,128)(2,1)} %bitcast.11), calls=%async_computation.4 | async-start | bytes 2359296 | tf_op jit(solution)/shard_map/all_to_all | solution.py:101
  27.7 6.7 %scatter_custom_fusion.1 = bf16[1152,2048]{1,0:T(8,128)(2,1)} fusion(s32[384]{0:T(512)S(1)} %fusion.27, bf16[384,2048]{1,0:T(8,128)(2,1)} %param.7, bf16[]{:T(256)} %constant.71.clone.1), kind=kCustom, calls=%fused_computation.13 | custom fusion | bytes 4719104 | tf_op jit(solution)/shard_map/scatter | solution.py:49
  34.4 19.3 %all-to-all-done.3 = bf16[8,144,512]{2,1,0:T(8,128)(2,1)S(1)} async-done(((bf16[8,144,512]{2,1,0:T(8,128)(2,1)}), bf16[8,144,512]{2,1,0:T(8,128)(2,1)S(1)}, u32[]{:S(2)}, u32[]{:S(2)}) %all-to-all-start.3) | async-done | bytes 1179680 | tf_op jit(solution)/shard_map/all_to_all | solution.py:101
  53.7 6.3 %all-to-all-start.1 = ((bf16[8,144,2048]{2,1,0:T(8,128)(2,1)}), bf16[8,144,2048]{2,1,0:T(8,128)(2,1)}, u32[]{:S(2)}, u32[]{:S(2)}) async-start(bf16[8,144,2048]{2,1,0:T(8,128)(2,1)} %bitcast.74), calls=%async_computation.2 | async-start | bytes 9437184 | tf_op jit(solution)/shard_map/all_to_all | solution.py:81
  60.8 1.5 fusion.2
  63.1 98.7 %all-to-all-done.1 = bf16[8,144,2048]{2,1,0:T(8,128)(2,1)} async-done(((bf16[8,144,2048]{2,1,0:T(8,128)(2,1)}), bf16[8,144,2048]{2,1,0:T(8,128)(2,1)}, u32[]{:S(2)}, u32[]{:S(2)}) %all-to-all-start.1) | async-done | bytes 4718624 | tf_op jit(solution)/shard_map/all_to_all | solution.py:81
  161.8 3.9 %convolution_select_fusion = f32[1152,256]{0,1:T(8,128)S(1)} fusion(bf16[1152,2048]{1,0:T(8,128)(2,1)} %bitcast.5, bf16[256,2048]{1,0:T(8,128)(2,1)S(1)} %bitcast.73, bf16[1152]{0:T(1024)(128)(2,1)S(1)} %eq.81, bf16[256]{0:T(256)(128)(2,1)S(1)} %fusion.28), kind=kOutput, calls=%fused_computation.12 | convolution fusion | flops 1208549376 | bytes 6949632 | tf_op jit(solution)/shard_map/dot_general | solution.py:10
  166.5 17.5 %all-reduce.2 = (bf16[1152,64]{0,1:T(8,128)(2,1)S(1)}, bf16[1152,64]{0,1:T(8,128)(2,1)S(1)}) all-reduce(f32[1152,64]{0,1:T(8,128)} %reduce_sum.47, f32[1152,64]{0,1:T(8,128)} %reduce_sum.48), channel_id=1, replica_groups=mesh['dp'=8,'tensor'=4] {'tensor'}, use_global_device_ids=true, to_apply=%region_8.9 | all-reduce | flops 147456 | bytes 884736 | tf_op jit(solution)/shard_map/psum | solution.py:89
  184.1 2.6 fusion.1
  186.7 6.8 %all-to-all-start.2 = ((bf16[8,144,512]{2,1,0:T(8,128)(2,1)}), bf16[8,144,512]{2,1,0:T(8,128)(2,1)S(1)}, u32[]{:S(2)}, u32[]{:S(2)}) async-start(bf16[8,144,512]{2,1,0:T(8,128)(2,1)} %bitcast.80), calls=%async_computation.3 | async-start | bytes 2359296 | tf_op jit(solution)/shard_map/all_to_all | solution.py:94
  193.5 10.0 %fusion.31 = f32[2048,384]{1,0:T(8,128)} fusion(bf16[2048,2048]{1,0:T(8,128)(2,1)} %param.8, bf16[384,2048]{1,0:T(8,128)(2,1)} %param.7), kind=kOutput, calls=%fused_computation.79 | convolution fusion | flops 3221225472 | bytes 13107200 | tf_op jit(solution)/shard_map/dot_general | solution.py:16
  203.6 4.4 %bitcast_convert_fusion = bf16[1152,2048]{1,0:T(8,128)(2,1)} fusion(bf16[4,64,2048]{2,1,0:T(8,128)(2,1)S(1)} %copy-done, bf16[1152,64]{0,1:T(8,128)(2,1)S(1)} %get-tuple-element.21, bf16[4,64]{1,0:T(4,128)(2,1)} %fusion.20, bf16[1152]{0:T(1024)(128)(2,1)} %copy-done.2), kind=kOutput, calls=%fused_computation.5 | convolution fusion | flops 1211498496 | bytes 5917440 | tf_op jit(solution)/shard_map/dot_general | solution.py:110
  208.0 11.6 %all-to-all-done.2 = bf16[8,144,512]{2,1,0:T(8,128)(2,1)S(1)} async-done(((bf16[8,144,512]{2,1,0:T(8,128)(2,1)}), bf16[8,144,512]{2,1,0:T(8,128)(2,1)S(1)}, u32[]{:S(2)}, u32[]{:S(2)}) %all-to-all-start.2) | async-done | bytes 1179680 | tf_op jit(solution)/shard_map/all_to_all | solution.py:94
  219.6 6.3 %all-to-all-start.4 = ((bf16[8,144,2048]{2,1,0:T(8,128)(2,1)}), bf16[8,144,2048]{2,1,0:T(8,128)(2,1)}, u32[]{:S(2)}, u32[]{:S(2)}) async-start(bf16[8,144,2048]{2,1,0:T(8,128)(2,1)} %bitcast.76), calls=%async_computation.5 | async-start | bytes 9437184 | tf_op jit(solution)/shard_map/all_to_all | solution.py:113
  229.9 1.3 convolution_multiply_fusion.1
  231.2 5.2 %fusion.32 = f32[4,64,2048]{2,1,0:T(8,128)} fusion(bf16[4,64,1152]{2,1,0:T(8,128)(2,1)S(1)} %bitcast.83, bf16[1152,2048,1]{1,0,2:T(8,128)(2,1)} %bitcast.21), kind=kOutput, calls=%fused_computation.80 | convolution fusion | flops 1207959552 | bytes 7405568 | tf_op jit(solution)/shard_map/dot_general | solution.py:16
  236.4 2.1 gather_fusion
  238.7 3.8 %reduce-scatter.2.cloned.1.call-done = f32[512,384]{1,0:T(8,128)} async-done(((f32[2048,384]{1,0:T(8,128)}), f32[512,384]{1,0:T(8,128)}) %reduce-scatter.2.cloned.1.call-update) | async-done | bytes 786448 | tf_op jit(solution)/shard_map/reduce_scatter | solution.py:129
  244.6 83.2 %all-to-all-done.4 = bf16[8,144,2048]{2,1,0:T(8,128)(2,1)} async-done(((bf16[8,144,2048]{2,1,0:T(8,128)(2,1)}), bf16[8,144,2048]{2,1,0:T(8,128)(2,1)}, u32[]{:S(2)}, u32[]{:S(2)}) %all-to-all-start.4) | async-done | bytes 4718624 | tf_op jit(solution)/shard_map/all_to_all | solution.py:113
  327.8 7.3 %gather_fusion.1 = bf16[384,2048]{1,0:T(8,128)(2,1)S(1)} fusion(bf16[1152,2048]{1,0:T(8,128)(2,1)} %bitcast.17, s32[1024]{0:T(1024)S(1)} %copy-done.3), kind=kCustom, calls=%fused_computation.1 | custom fusion | bytes 3147264 | tf_op jit(solution)/shard_map/gather | solution.py:127
  335.2 8.5 %add_convert_fusion = bf16[384,2048]{1,0:T(8,128)(2,1)} fusion(bf16[384,2048]{1,0:T(8,128)(2,1)S(1)} %gather_fusion.1, bf16[384,2048]{1,0:T(8,128)(2,1)} %all-gather.2.cloned.1.call-done, bf16[2048,2048]{1,0:T(8,128)(2,1)} %param.8), kind=kOutput, calls=%fused_computation.8 | convolution fusion | flops 3223584768 | bytes 13107200 | tf_op jit(solution)/shard_map/dot_general | solution.py:10
  (40 shorter events, 11.5 us)
Async XLA Ops:
  7.2 154.6 %copy-start = (bf16[4,64,2048]{2,1,0:T(8,128)(2,1)S(1)}, bf16[4,64,2048]{2,1,0:T(8,128)(2,1)}, u32[]{:S(2)}) copy-start(bf16[4,64,2048]{2,1,0:T(8,128)(2,1)} %param.9) | copy-start | bytes 3145732
  9.3 18.3 %copy-start.4 = (s32[384]{0:T(512)}, s32[384]{0:T(512)S(1)}, u32[]{:S(2)}) copy-start(s32[384]{0:T(512)S(1)} %fusion.27) | copy-start | bytes 4612
  13.0 9.2 %all-to-all-start = ((bf16[8,1,144]{2,1,0:T(2,128)(2,1)}), bf16[8,1,144]{2,1,0:T(2,128)(2,1)S(1)}, u32[]{:S(2)}, u32[]{:S(2)}) async-start(bf16[8,1,144]{2,1,0:T(2,128)(2,1)} %all_to_all.24), calls=%async_computation.1 | async-start | bytes 16384 | tf_op jit(solution)/shard_map/all_to_all | solution.py:82
  22.2 31.4 %all-to-all-start.3 = ((bf16[8,144,512]{2,1,0:T(8,128)(2,1)}), bf16[8,144,512]{2,1,0:T(8,128)(2,1)S(1)}, u32[]{:S(2)}, u32[]{:S(2)}) async-start(bf16[8,144,512]{2,1,0:T(8,128)(2,1)} %bitcast.11), calls=%async_computation.4 | async-start | bytes 2359296 | tf_op jit(solution)/shard_map/all_to_all | solution.py:101
  53.7 108.1 %all-to-all-start.1 = ((bf16[8,144,2048]{2,1,0:T(8,128)(2,1)}), bf16[8,144,2048]{2,1,0:T(8,128)(2,1)}, u32[]{:S(2)}, u32[]{:S(2)}) async-start(bf16[8,144,2048]{2,1,0:T(8,128)(2,1)} %bitcast.74), calls=%async_computation.2 | async-start | bytes 9437184 | tf_op jit(solution)/shard_map/all_to_all | solution.py:81
  60.0 101.8 %copy-start.5 = (bf16[256]{0:T(256)(128)(2,1)}, bf16[256]{0:T(256)(128)(2,1)S(1)}, u32[]{:S(2)}) copy-start(bf16[256]{0:T(256)(128)(2,1)S(1)} %fusion.28) | copy-start | bytes 1540
  60.8 101.0 %copy-start.2 = (bf16[1152]{0:T(1024)(128)(2,1)}, bf16[1152]{0:T(1024)(128)(2,1)S(1)}, u32[]{:S(2)}) copy-start(bf16[1152]{0:T(1024)(128)(2,1)S(1)} %eq.81) | copy-start | bytes 6916
  184.0 2.6 copy-start.1
  186.7 32.9 %all-to-all-start.2 = ((bf16[8,144,512]{2,1,0:T(8,128)(2,1)}), bf16[8,144,512]{2,1,0:T(8,128)(2,1)S(1)}, u32[]{:S(2)}, u32[]{:S(2)}) async-start(bf16[8,144,512]{2,1,0:T(8,128)(2,1)} %bitcast.80), calls=%async_computation.3 | async-start | bytes 2359296 | tf_op jit(solution)/shard_map/all_to_all | solution.py:94
  193.5 49.0 %reduce-scatter.2.cloned.1.call-start = ((), (), s32[]{:S(2)}) async-start(), calls=%async_computation.6 | async-start | bytes 3932160 | tf_op jit(solution)/shard_map/reduce_scatter | solution.py:129
  219.6 108.2 %all-to-all-start.4 = ((bf16[8,144,2048]{2,1,0:T(8,128)(2,1)}), bf16[8,144,2048]{2,1,0:T(8,128)(2,1)}, u32[]{:S(2)}, u32[]{:S(2)}) async-start(bf16[8,144,2048]{2,1,0:T(8,128)(2,1)} %bitcast.76), calls=%async_computation.5 | async-start | bytes 9437184 | tf_op jit(solution)/shard_map/all_to_all | solution.py:113
  225.9 109.3 %all-gather.2.cloned.1.call-start = ((), (), s32[]{:S(2)}) async-start(), calls=%async_computation.7 | async-start | bytes 1966080 | tf_op jit(solution)/shard_map/all_gather | solution.py:78
  231.2 5.2 %copy-start.3 = (s32[1024]{0:T(1024)S(1)}, s32[1024]{0:T(1024)}, u32[]{:S(2)}) copy-start(s32[1024]{0:T(1024)} %pad_clamp_fusion) | copy-start | bytes 12292
Sparse Core Ops, SparseCore 0:
  203.7 38.7 reduce-scatter.1
  244.0 20.1 all-gather.1
where the time goes:
time: 356 us; the launch traced here: 350 us
  waiting for transfers between devices  217 us (61%)
  matrix products  37.4 us (11%)
  starting transfers between devices  30.6 us (9%)
  local copies, waits for them, and re-layouts  24.8 us (7%)
  blocking collectives  17.5 us (5%)
  between operations  14.2 us (4%)
  other arithmetic  8.58 us (2%)
    all_to_all x1, waiting for transfers between devices, body(): lax.all_to_all(to_buffer(features), 'dp', split_axis=0, concat_axis=0, ti...  98.7 us
    all_to_all x1, waiting for transfers between devices, body(): lax.all_to_all(input_row_block.reshape(token_groups, row_capacity, width_...  83.2 us
    all_to_all x1, waiting for transfers between devices, body(): lax.all_to_all(to_buffer(output_gradient), 'dp', split_axis=0, concat_axi...  19.3 us
    psum x1, blocking collectives, body(): down_total = lax.psum(down_part, 'tensor')  17.5 us
    dot_general x3, matrix products, contract_leading(): lax.dot_general(left, right, (((0,), (0,)), ((), ())), preferred_element_...  16.6 us
    dot_general x3, matrix products, contract_trailing(): lax.dot_general(left, right, (((1,), (1,)), ((), ())), preferred_element_...  13.8 us
    all_to_all x1, waiting for transfers between devices, body(): lax.all_to_all(adapter_row_block.reshape(token_groups, row_capacity, outp...  11.6 us
    scatter x2, local copies, waits for them, and re-layouts, to_buffer(): jnp.zeros((holding_rows, source.shape[1]), source.dtype).at[target_slot]  10.3 us
  transfers between devices with their start and end apart: 7, of which 5 were waited for; matrix products, arithmetic and copies ran while one was open for 14% of the time, Pallas kernels for 0%

commit v1 on v0

v1 whole, which is shorter than its diff:
```python
import functools

import jax
import jax.numpy as jnp
from jax import lax
from jax.experimental import pallas as pl
from jax.experimental.pallas import tpu as pltpu
from jax.sharding import PartitionSpec as P

adapter_scale = 2.0


def dot_dims(left, right, left_dim, right_dim):
    return lax.dot_general(
        left, right, (((left_dim,), (right_dim,)), ((), ())), preferred_element_type=jnp.float32
    )


def slot_mask(slot_row, rank, rows):
    tokens = slot_row.shape[1]
    row_slot = lax.broadcasted_iota(jnp.int32, (rows, tokens), 0) // rank
    return row_slot == slot_row


def project_kernel(rank, scale, slot_ref, x_ref, w_ref, o_ref):
    rows = w_ref.shape[0]
    full = dot_dims(w_ref[...], x_ref[...], 1, 1)
    kept = jnp.where(slot_mask(slot_ref[...], rank, rows), full, 0.0)
    o_ref[0] = scale * jnp.sum(kept.reshape(rows // rank, rank, kept.shape[1]), axis=0)


def widen(values, slot_row, rows):
    rank = values.shape[0]
    tiled = jnp.tile(values.astype(jnp.float32), (rows // rank, 1))
    return jnp.where(slot_mask(slot_row, rank, rows), tiled, 0.0).astype(jnp.bfloat16)


def back_kernel(slot_ref, up_ref, x_ref, w_ref, rows_ref, grad_ref, total):
    step = pl.program_id(0)
    wide = widen(up_ref[0], slot_ref[...], w_ref.shape[0])
    rows_ref[...] = dot_dims(wide, w_ref[...], 0, 0).astype(rows_ref.dtype)
    part = jnp.dot(wide, x_ref[...], preferred_element_type=jnp.float32)

    @pl.when(step == 0)
    def _():
        total[...] = part

    @pl.when(step > 0)
    def _():
        total[...] += part

    @pl.when(step == pl.num_programs(0) - 1)
    def _():
        grad_ref[...] = total[...].astype(grad_ref.dtype)


def up_grad_kernel(slot_ref, down_ref, dy_ref, grad_ref, total):
    step = pl.program_id(0)
    wide = widen(down_ref[0], slot_ref[...], grad_ref.shape[1])
    part = dot_dims(dy_ref[...], wide, 1, 1)

    @pl.when(step == 0)
    def _():
        total[...] = part

    @pl.when(step > 0)
    def _():
        total[...] += part

    @pl.when(step == pl.num_programs(0) - 1)
    def _():
        grad_ref[...] = (adapter_scale * total[...]).astype(grad_ref.dtype)


def out_kernel(slot_ref, down_ref, w_ref, base_ref, o_ref):
    wide = widen(down_ref[...], slot_ref[...], w_ref.shape[0])
    rows = (adapter_scale * dot_dims(wide, w_ref[...], 0, 0)).astype(jnp.bfloat16)
    o_ref[...] = (base_ref[...] + rows.astype(jnp.float32)).astype(o_ref.dtype)


def cost(flops, nbytes):
    return pl.CostEstimate(flops=int(flops), bytes_accessed=int(nbytes), transcendentals=0)


def project(slots, x, w, rank, tokens, scale, name):
    total_tokens, width = x.shape
    rows = w.shape[0]
    blocks = total_tokens // tokens
    return pl.pallas_call(
        functools.partial(project_kernel, rank, scale),
        out_shape=jax.ShapeDtypeStruct((blocks, rank, tokens), jnp.float32),
        grid=(blocks,),
        in_specs=[
            pl.BlockSpec((1, tokens), lambda i: (0, i)),
            pl.BlockSpec((tokens, width), lambda i: (i, 0)),
            pl.BlockSpec((rows, width), lambda i: (0, 0)),
        ],
        out_specs=pl.BlockSpec((1, rank, tokens), lambda i: (i, 0, 0)),
        cost_estimate=cost(2 * total_tokens * rows * width, 2 * (total_tokens + rows) * width),
        name=name,
    )(slots, x, w)


def back(slots, up_all, x, w, tokens):
    total_tokens, width = x.shape
    rows = w.shape[0]
    rank = up_all.shape[1]
    blocks = total_tokens // tokens
    return pl.pallas_call(
        back_kernel,
        out_shape=(
            jax.ShapeDtypeStruct((total_tokens, width), jnp.bfloat16),
            jax.ShapeDtypeStruct((rows, width), jnp.bfloat16),
        ),
        grid=(blocks,),
        in_specs=[
            pl.BlockSpec((1, tokens), lambda i: (0, i)),
            pl.BlockSpec((1, rank, tokens), lambda i: (i, 0, 0)),
            pl.BlockSpec((tokens, width), lambda i: (i, 0)),
            pl.BlockSpec((rows, width), lambda i: (0, 0)),
        ],
        out_specs=(
            pl.BlockSpec((tokens, width), lambda i: (i, 0)),
            pl.BlockSpec((rows, width), lambda i: (0, 0)),
        ),
        scratch_shapes=[pltpu.VMEM((rows, width), jnp.float32)],
        cost_estimate=cost(4 * total_tokens * rows * width, 4 * (total_tokens + rows) * width),
        name="back",
    )(slots, up_all, x, w)


def up_grad(slots, down_all, dy, rows, tokens):
    width, total_tokens = dy.shape
    rank = down_all.shape[1]
    blocks = total_tokens // tokens
    return pl.pallas_call(
        up_grad_kernel,
        out_shape=jax.ShapeDtypeStruct((width, rows), jnp.bfloat16),
        grid=(blocks,),
        in_specs=[
            pl.BlockSpec((1, tokens), lambda i: (0, i)),
            pl.BlockSpec((1, rank, tokens), lambda i: (i, 0, 0)),
            pl.BlockSpec((width, tokens), lambda i: (0, i)),
        ],
        out_specs=pl.BlockSpec((width, rows), lambda i: (0, 0)),
        scratch_shapes=[pltpu.VMEM((width, rows), jnp.float32)],
        cost_estimate=cost(2 * total_tokens * rows * width, 2 * (total_tokens + rows) * width),
        name="up_grad",
    )(slots, down_all, dy)


def add_out(slots, down, w, base):
    tokens, width = base.shape
    return pl.pallas_call(
        out_kernel,
        out_shape=jax.ShapeDtypeStruct((tokens, width), jnp.bfloat16),
        cost_estimate=cost(2 * tokens * w.shape[0] * width, 2 * w.shape[0] * width),
        name="add_out",
    )(slots, down, w, base)


def body(
    features,
    key_value_weight,
    adapter_down_weight,
    adapter_up_weight,
    token_adapter_index,
    adapter_position,
    output_gradient,
):
    tokens, width_local = features.shape
    output_local = output_gradient.shape[1]
    local_count, rank, _ = adapter_down_weight.shape
    all_count = adapter_position.shape[0]
    down_matrix = adapter_down_weight.reshape(local_count * rank, width_local)
    up_matrix = adapter_up_weight.reshape(local_count * rank, output_local)

    def exchange(array, split, concat):
        return lax.all_to_all(array, "dp", split_axis=split, concat_axis=concat, tiled=True)

    up_rows = lax.all_gather(up_matrix, "dp", axis=0, tiled=True)
    ids = jnp.arange(all_count, dtype=jnp.int32)
    matches = token_adapter_index[:, None] == ids[None, :]
    slot_tok = jnp.sum(jnp.where(matches, adapter_position[None, :], 0), axis=1)
    slots = slot_tok.reshape(1, tokens)
    slots_all = lax.all_gather(slot_tok, "dp", axis=0, tiled=True).reshape(1, -1)

    down_cols = exchange(down_matrix, 1, 0)
    feature_cols = exchange(features, 1, 0)
    dy_cols = exchange(output_gradient.T, 0, 1)

    up_part = project(slots, output_gradient, up_rows, rank, tokens, adapter_scale, "up_back")
    up_own = lax.psum(up_part[0], "tensor").astype(jnp.bfloat16)
    up_all = lax.all_gather(up_own, "dp", axis=0, tiled=False)

    down_part = project(slots_all, feature_cols, down_cols, rank, tokens, 1.0, "down")
    down_all = lax.psum(down_part, ("dp", "tensor")).astype(jnp.bfloat16)

    in_cols, down_grad_cols = back(slots_all, up_all, feature_cols, down_cols, tokens)
    lora_in = exchange(in_cols, 0, 1)
    down_gradient = exchange(down_grad_cols, 0, 1)

    up_grad_cols = up_grad(slots_all, down_all, dy_cols, all_count * rank, tokens)
    up_gradient = exchange(up_grad_cols, 1, 0)

    gradient_frozen = dot_dims(
        lax.all_gather(output_gradient, "tensor", axis=1, tiled=True), key_value_weight, 1, 1
    )
    key_value_frozen = lax.psum_scatter(
        dot_dims(key_value_weight, features, 0, 1), "tensor", scatter_dimension=0, tiled=True
    ).T
    down_own = lax.dynamic_index_in_dim(down_all, lax.axis_index("dp"), 0, keepdims=False)
    key_value_output = add_out(slots, down_own, up_rows, key_value_frozen)
    feature_gradient = (gradient_frozen + lora_in.astype(jnp.float32)).astype(jnp.bfloat16)
    return (
        key_value_output,
        feature_gradient,
        down_gradient.astype(jnp.float32).reshape(local_count, rank, width_local),
        up_gradient.astype(jnp.float32).T.reshape(local_count, rank, output_local),
    )


def solution(mesh):
    placed = (
        P("dp", "tensor"),
        P("tensor", None),
        P("dp", None, "tensor"),
        P("dp", None, "tensor"),
        P("dp"),
        P(),
        P("dp", "tensor"),
    )
    return jax.shard_map(
        body,
        mesh=mesh,
        in_specs=placed,
        out_specs=(
            P("dp", "tensor"),
            P("dp", "tensor"),
            P("dp", None, "tensor"),
            P("dp", None, "tensor"),
        ),
        check_vma=False,
    )
```

time: 356 us -> 357 us (level)
  waiting for transfers between devices: 217 us -> 76.7 us
  blocking collectives: 17.5 us -> 157 us
  Pallas kernels: 0 us -> 36.9 us
  matrix products: 37.4 us -> 16.9 us
  local copies, waits for them, and re-layouts: 24.8 us -> 16 us
  other arithmetic: 8.58 us -> 1.99 us
    all_to_all x5, waiting for transfers between devices: 213 us -> 75.4 us  [exchange(): lax.all_to_all(array, 'dp', split_axis=split, concat_axis=concat, tiled=T...]
    all_gather x0 -> x2, blocking collectives: none -> 61.2 us  [the longest x1 37.1 us: body(): lax.all_gather(slot_tok, 'dp', axis=0, tiled=True).reshape(1, -1)]
    psum x1 -> x2, blocking collectives: 17.5 us -> 67.6 us  [the longest x1 54.3 us: body(): down_all = lax.psum(down_part, ('dp', 'tensor')).astype(jnp.bfloat16)]
    pallas_call x0 -> x5, Pallas kernels: none -> 36.9 us  [the longest x1 13.5 us: back(): pl.pallas_call(back_kernel, out_shape=(jax.ShapeDtypeStruct((total_tokens...]
    all_to_all x0 -> x1, blocking collectives: none -> 28.5 us  [exchange(): lax.all_to_all(array, 'dp', split_axis=split, concat_axis=concat, tiled=T...]
    dot_general x8 -> x2, matrix products: 37.4 us -> 16.9 us  [dot_dims(): lax.dot_general(left, right, (((left_dim,), (right_dim,)), ((), ())), pre...]
    scatter x3 -> x0, local copies, waits for them, and re-layouts: 13.2 us -> none  [the longest x2 10.3 us: to_buffer(): jnp.zeros((holding_rows, source.shape[1]), source.dtype).at[target_slot]]
    gather x3 -> x0, local copies, waits for them, and re-layouts: 9.6 us -> none  [the longest x1 7.34 us: body(): input_tok = input_back.reshape(holding_rows, width_local)[target_slot]]
  transfers between devices with their start and end apart: 7 -> 8, of which waited for: 5 -> 3; matrix products, arithmetic and copies ran while one was open for 14% -> 7% of each run, Pallas kernels for 0% -> 11%
where the time goes in v1:
time: 357 us; the launch traced here: 351 us
  blocking collectives  157 us (44%)
  waiting for transfers between devices  76.7 us (21%)
  Pallas kernels  36.9 us (10%)
  starting transfers between devices  29.6 us (8%)
  matrix products  16.9 us (5%)
  local copies, waits for them, and re-layouts  16 us (4%)
  between operations  15.6 us (4%)
    all_to_all x5, waiting for transfers between devices, exchange(): lax.all_to_all(array, 'dp', split_axis=split, concat_axis=concat, tiled=T...  75.4 us
    psum x1, blocking collectives, body(): down_all = lax.psum(down_part, ('dp', 'tensor')).astype(jnp.bfloat16)  54.3 us
    all_gather x1, blocking collectives, body(): lax.all_gather(slot_tok, 'dp', axis=0, tiled=True).reshape(1, -1)  37.1 us
    all_to_all x5, starting transfers between devices, exchange(): lax.all_to_all(array, 'dp', split_axis=split, concat_axis=concat, tiled=T...  29.6 us
    all_to_all x1, blocking collectives, exchange(): lax.all_to_all(array, 'dp', split_axis=split, concat_axis=concat, tiled=T...  28.5 us
    all_gather x1, blocking collectives, body(): up_all = lax.all_gather(up_own, 'dp', axis=0, tiled=False)  24.2 us
    dot_general x2, matrix products, dot_dims(): lax.dot_general(left, right, (((left_dim,), (right_dim,)), ((), ())), pre...  16.9 us
    pallas_call x1, Pallas kernels, back(): pl.pallas_call(back_kernel, out_shape=(jax.ShapeDtypeStruct((total_tokens...  13.5 us
  transfers between devices with their start and end apart: 8, of which 3 were waited for; matrix products, arithmetic and copies ran while one was open for 7% of the time, Pallas kernels for 11%

profile of v1, /device:TPU:11, one launch (start us, length us, event | category | flops | bytes accessed | tf_op | source)
XLA Modules:
  0.0 351.0 jit_solution(12780262355048613271)
XLA Ops:
  8.7 1.9 copy.49
  10.7 5.7 %all-to-all-start.4 = ((bf16[8,64,384]{2,1,0:T(8,128)(2,1)}), bf16[8,64,384]{2,1,0:T(8,128)(2,1)S(1)}, u32[]{:S(2)}, u32[]{:S(2)}) async-start(bf16[8,64,384]{2,1,0:T(8,128)(2,1)} %bitcast.17), calls=%async_computation.5 | async-start | bytes 786432 | tf_op jit(solution)/shard_map/all_to_all | solution.py:179
  17.8 11.6 %all-to-all-done.4 = bf16[8,64,384]{2,1,0:T(8,128)(2,1)S(1)} async-done(((bf16[8,64,384]{2,1,0:T(8,128)(2,1)}), bf16[8,64,384]{2,1,0:T(8,128)(2,1)S(1)}, u32[]{:S(2)}, u32[]{:S(2)}) %all-to-all-start.4) | async-done | bytes 393248 | tf_op jit(solution)/shard_map/all_to_all | solution.py:179
  29.4 7.1 %all-to-all-start.1 = ((bf16[256,8,256]{2,0,1:T(8,128)(2,1)}), bf16[256,8,256]{2,0,1:T(8,128)(2,1)S(1)}, u32[]{:S(2)}, u32[]{:S(2)}) async-start(bf16[256,8,256]{2,0,1:T(8,128)(2,1)} %copy.45), calls=%async_computation.1 | async-start | bytes 2097152 | tf_op jit(solution)/shard_map/all_to_all | solution.py:179
  37.8 38.8 %all-to-all-done.1 = bf16[256,8,256]{2,0,1:T(8,128)(2,1)S(1)} async-done(((bf16[256,8,256]{2,0,1:T(8,128)(2,1)}), bf16[256,8,256]{2,0,1:T(8,128)(2,1)S(1)}, u32[]{:S(2)}, u32[]{:S(2)}) %all-to-all-start.1) | async-done | bytes 1048608 | tf_op jit(solution)/shard_map/all_to_all | solution.py:179
  77.6 6.3 %all-to-all-start = ((bf16[384,8,256]{2,0,1:T(8,128)(2,1)}), bf16[384,8,256]{2,0,1:T(8,128)(2,1)S(1)}, u32[]{:S(2)}, u32[]{:S(2)}) async-start(bf16[384,8,256]{2,0,1:T(8,128)(2,1)} %bitcast.46), calls=%async_computation | async-start | bytes 3145728 | tf_op jit(solution)/shard_map/all_to_all | solution.py:179
  84.0 8.4 %fusion = f32[2048,384]{0,1:T(8,128)} fusion(bf16[384,2048]{1,0:T(8,128)(2,1)S(1)} %copy-done, bf16[2048,2048]{1,0:T(8,128)(2,1)} %param.8), kind=kOutput, calls=%fused_computation.8 | convolution fusion | flops 3221225472 | bytes 13107200 | tf_op jit(solution)/shard_map/dot_general | solution.py:14
  93.7 37.1 %all-gather.1 = s32[8,1,384]{2,1,0:T(1,128)} all-gather(s32[1,1,384]{2,1,0:T(1,128)S(1)} %reshape.67), channel_id=1, replica_groups=mesh['dp'=8,'tensor'=4] {'dp'}, dimensions={0}, use_global_device_ids=true | all-gather | bytes 13824 | tf_op jit(solution)/shard_map/all_gather | solution.py:186
  132.7 8.7 %down.1 = f32[8,64,384]{2,1,0:T(8,128)} custom-call(s32[1,3072]{1,0:T(1,128)} %bitcast.66, bf16[3072,256]{1,0:T(8,128)(2,1)} %bitcast.52, bf16[2048,256]{1,0:T(8,128)(2,1)} %bitcast.56), custom_call_target="tpu_custom_call" | custom-call | flops 3221225472 | bytes 2621440 | tf_op jit(solution)/shard_map/down/pallas_call | solution.py:89
  141.4 54.3 %all-reduce.1.down_ref = bf16[8,64,384]{2,1,0:T(8,128)(2,1)} all-reduce(f32[8,64,384]{2,1,0:T(8,128)} %down.1), channel_id=1, replica_groups=mesh['dp'=8,'tensor'=4] {'dp','tensor'}, use_global_device_ids=true, to_apply=%region_1.2 | all-reduce | flops 196608 | bytes 1179648 | tf_op jit(solution)/shard_map/psum | solution.py:197
  195.7 7.5 %up_grad.1 = bf16[64,2048]{1,0:T(8,128)(2,1)} custom-call(s32[1,3072]{1,0:T(1,128)} %bitcast.67, bf16[8,64,384]{2,1,0:T(8,128)(2,1)} %all-reduce.1.down_ref, bf16[64,3072]{1,0:T(8,128)(2,1)} %bitcast.61), custom_call_target="tpu_custom_call" | custom-call | flops 805306368 | bytes 655360 | tf_op jit(solution)/shard_map/up_grad/pallas_call | solution.py:136
  203.2 1.7 copy.62
  204.8 4.0 %all-to-all-start.5 = ((bf16[64,8,256]{2,0,1:T(8,128)(2,1)}), bf16[64,8,256]{2,0,1:T(8,128)(2,1)S(1)}, u32[]{:S(2)}, u32[]{:S(2)}) async-start(bf16[64,8,256]{2,0,1:T(8,128)(2,1)} %bitcast.47), calls=%async_computation.6 | async-start | bytes 524288 | tf_op jit(solution)/shard_map/all_to_all | solution.py:179
  208.8 3.6 %up_back.1 = f32[1,64,384]{2,1,0:T(8,128)} custom-call(s32[1,384]{1,0:T(1,128)} %reshape.53.slot_ref, bf16[384,512]{1,0:T(8,128)(2,1)} %x_ref.1, bf16[2048,512]{1,0:T(8,128)(2,1)} %all-gather.5.cloned.1.call-done.w_ref), custom_call_target="tpu_custom_call" | custom-call | flops 805306368 | bytes 2490368 | tf_op jit(solution)/shard_map/up_back/pallas_call | solution.py:89
  212.5 13.4 %psum.15 = bf16[64,384]{1,0:T(8,128)(2,1)S(1)} all-reduce(f32[64,384]{1,0:T(8,128)} %bitcast.65), channel_id=1, replica_groups=mesh['dp'=8,'tensor'=4] {'tensor'}, use_global_device_ids=true, to_apply=%region_3.4 | all-reduce | flops 24576 | bytes 147456 | tf_op jit(solution)/shard_map/psum | solution.py:193
  225.9 24.2 %all-gather = bf16[512,384]{1,0:T(8,128)(2,1)} all-gather(bf16[64,384]{1,0:T(8,128)(2,1)S(1)} %psum.15), channel_id=2, replica_groups=mesh['dp'=8,'tensor'=4] {'dp'}, dimensions={0}, use_global_device_ids=true | all-gather | bytes 442368 | tf_op jit(solution)/shard_map/all_gather | solution.py:194
  250.0 13.5 %back.1 = (bf16[3072,256]{1,0:T(8,128)(2,1)}, bf16[2048,256]{1,0:T(8,128)(2,1)}) custom-call(s32[1,3072]{1,0:T(1,128)} %bitcast.68, bf16[8,64,384]{2,1,0:T(8,128)(2,1)} %bitcast.62, bf16[3072,256]{1,0:T(8,128)(2,1)} %bitcast.53, bf16[2048,256]{1,0:T(8,128)(2,1)} %bitcast.57), custom_call_target="tpu_custom_call" | custom-call | flops 6442450944 | bytes 5242880 | tf_op jit(solution)/shard_map/back/pallas_call | solution.py:109
  263.6 28.5 %all_to_all.96 = bf16[8,256,256]{2,1,0:T(8,128)(2,1)S(1)} all-to-all(bf16[8,256,256]{2,1,0:T(8,128)(2,1)} %bitcast.58), channel_id=1, replica_groups=mesh['dp'=8,'tensor'=4] {'dp'}, dimensions={0} | all-to-all | bytes 2097152 | tf_op jit(solution)/shard_map/all_to_all | solution.py:179
  292.1 6.4 %all-to-all-start.2 = ((bf16[8,384,256]{2,1,0:T(8,128)(2,1)}), bf16[8,384,256]{2,1,0:T(8,128)(2,1)}, u32[]{:S(2)}, u32[]{:S(2)}) async-start(bf16[8,384,256]{2,1,0:T(8,128)(2,1)} %bitcast.12), calls=%async_computation.3 | async-start | bytes 3145728 | tf_op jit(solution)/shard_map/all_to_all | solution.py:179
  303.0 1.5 reshape.59
  304.5 3.6 %add_out.1 = bf16[384,512]{1,0:T(8,128)(2,1)} custom-call(s32[1,384]{1,0:T(1,128)} %reshape.53.slot_ref, bf16[64,384]{1,0:T(8,128)(2,1)} %dynamic-slice_bitcast_fusion.down_ref, bf16[2048,512]{1,0:T(8,128)(2,1)} %all-gather.5.cloned.1.call-done.w_ref, f32[384,512]{1,0:T(8,128)} %bitcast.59), custom_call_target="tpu_custom_call" | custom-call | flops 805306368 | bytes 2097152 | tf_op jit(solution)/shard_map/add_out/pallas_call | solution.py:154
  308.1 24.9 %all-to-all-done.2 = bf16[8,384,256]{2,1,0:T(8,128)(2,1)} async-done(((bf16[8,384,256]{2,1,0:T(8,128)(2,1)}), bf16[8,384,256]{2,1,0:T(8,128)(2,1)}, u32[]{:S(2)}, u32[]{:S(2)}) %all-to-all-start.2) | async-done | bytes 1572896 | tf_op jit(solution)/shard_map/all_to_all | solution.py:179
  333.0 1.7 convert_bitcast_fusion
  335.1 8.5 %add_convert_fusion = bf16[384,2048]{1,0:T(8,128)(2,1)} fusion(f32[384,2048]{1,0:T(8,128)S(1)} %bitcast.49, bf16[384,2048]{1,0:T(8,128)(2,1)} %all-gather.7.cloned.1.call-done, bf16[2048,2048]{1,0:T(8,128)(2,1)} %param.8), kind=kOutput, calls=%fused_computation.1 | convolution fusion | flops 3222798336 | bytes 14680064 | tf_op jit(solution)/shard_map/dot_general | solution.py:14
  (36 shorter events, 12.6 us)
Async XLA Ops:
  8.0 8.3 %copy-start.2 = (bf16[4,64,2048]{2,1,0:T(8,128)(2,1)S(1)}, bf16[4,64,2048]{2,1,0:T(8,128)(2,1)}, u32[]{:S(2)}) copy-start(bf16[4,64,2048]{2,1,0:T(8,128)(2,1)} %param.9) | copy-start | bytes 3145732
  8.0 200.8 %all-gather.5.cloned.1.call-start = ((), (), s32[]{:S(2)}) async-start(), calls=%async_computation.7 | async-start | bytes 2359296 | tf_op jit(solution)/shard_map/all_gather | solution.py:181
  10.7 18.8 %all-to-all-start.4 = ((bf16[8,64,384]{2,1,0:T(8,128)(2,1)}), bf16[8,64,384]{2,1,0:T(8,128)(2,1)S(1)}, u32[]{:S(2)}, u32[]{:S(2)}) async-start(bf16[8,64,384]{2,1,0:T(8,128)(2,1)} %bitcast.17), calls=%async_computation.5 | async-start | bytes 786432 | tf_op jit(solution)/shard_map/all_to_all | solution.py:179
  16.6 19.9 %copy-start = (bf16[384,2048]{1,0:T(8,128)(2,1)S(1)}, bf16[384,2048]{1,0:T(8,128)(2,1)}, u32[]{:S(2)}) copy-start(bf16[384,2048]{1,0:T(8,128)(2,1)} %param.7) | copy-start | bytes 4718596
  29.4 47.2 %all-to-all-start.1 = ((bf16[256,8,256]{2,0,1:T(8,128)(2,1)}), bf16[256,8,256]{2,0,1:T(8,128)(2,1)S(1)}, u32[]{:S(2)}, u32[]{:S(2)}) async-start(bf16[256,8,256]{2,0,1:T(8,128)(2,1)} %copy.45), calls=%async_computation.1 | async-start | bytes 2097152 | tf_op jit(solution)/shard_map/all_to_all | solution.py:179
  76.6 1.0 copy-start.3
  77.6 53.9 %all-to-all-start = ((bf16[384,8,256]{2,0,1:T(8,128)(2,1)}), bf16[384,8,256]{2,0,1:T(8,128)(2,1)S(1)}, u32[]{:S(2)}, u32[]{:S(2)}) async-start(bf16[384,8,256]{2,0,1:T(8,128)(2,1)} %bitcast.46), calls=%async_computation | async-start | bytes 3145728 | tf_op jit(solution)/shard_map/all_to_all | solution.py:179
  84.0 220.5 %reduce-scatter.2.cloned.1.call-start = ((), (), s32[]{:S(2)}) async-start(), calls=%async_computation.8 | async-start | bytes 3932160 | tf_op jit(solution)/shard_map/reduce_scatter | solution.py:209
  92.4 0.7 copy-start.4
  92.4 0.7 copy-start.5
  131.6 1.1 copy-start.1
  204.8 58.7 %all-to-all-start.5 = ((bf16[64,8,256]{2,0,1:T(8,128)(2,1)}), bf16[64,8,256]{2,0,1:T(8,128)(2,1)S(1)}, u32[]{:S(2)}, u32[]{:S(2)}) async-start(bf16[64,8,256]{2,0,1:T(8,128)(2,1)} %bitcast.47), calls=%async_computation.6 | async-start | bytes 524288 | tf_op jit(solution)/shard_map/all_to_all | solution.py:179
  292.1 40.9 %all-to-all-start.2 = ((bf16[8,384,256]{2,1,0:T(8,128)(2,1)}), bf16[8,384,256]{2,1,0:T(8,128)(2,1)}, u32[]{:S(2)}, u32[]{:S(2)}) async-start(bf16[8,384,256]{2,1,0:T(8,128)(2,1)} %bitcast.12), calls=%async_computation.3 | async-start | bytes 3145728 | tf_op jit(solution)/shard_map/all_to_all | solution.py:179
  298.5 36.6 %all-gather.7.cloned.1.call-start = ((), (), s32[]{:S(2)}) async-start(), calls=%async_computation.9 | async-start | bytes 1966080 | tf_op jit(solution)/shard_map/all_gather | solution.py:207
Sparse Core Ops, SparseCore 0:
  10.9 64.3 all-gather.4
Sparse Core Ops, SparseCore 1:
  92.5 38.8 reduce-scatter.1
  300.6 23.7 all-gather.6

commit v2 on v1

--- a/solution.py
+++ b/solution.py
@@ -22,11 +22,20 @@
     return row_slot == slot_row
 
 
-def project_kernel(rank, scale, slot_ref, x_ref, w_ref, o_ref):
-    rows = w_ref.shape[0]
+def fold_slots(full, slot_row, rank):
+    rows, tokens = full.shape
+    kept = jnp.where(slot_mask(slot_row, rank, rows), full, 0.0)
+    return jnp.sum(kept.reshape(rows // rank, rank, tokens), axis=0)
+
+
+def down_kernel(rank, slot_ref, x_ref, w_ref, o_ref):
     full = dot_dims(w_ref[...], x_ref[...], 1, 1)
-    kept = jnp.where(slot_mask(slot_ref[...], rank, rows), full, 0.0)
-    o_ref[0] = scale * jnp.sum(kept.reshape(rows // rank, rank, kept.shape[1]), axis=0)
+    o_ref[0] = fold_slots(full, slot_ref[...], rank).astype(o_ref.dtype)
+
+
+def up_kernel(rank, slot_ref, dy_ref, w_ref, o_ref):
+    full = dot_dims(w_ref[...], dy_ref[0, : w_ref.shape[0]], 0, 0)
+    o_ref[0] = (adapter_scale * fold_slots(full, slot_ref[...], rank)).astype(o_ref.dtype)
 
 
 def widen(values, slot_row, rows):
@@ -54,10 +63,13 @@
         grad_ref[...] = total[...].astype(grad_ref.dtype)
 
 
-def up_grad_kernel(slot_ref, down_ref, dy_ref, grad_ref, total):
+def up_grad_kernel(slot_ref, down_ref, dy_ref, w_ref, rows_ref, grad_ref, total):
     step = pl.program_id(0)
-    wide = widen(down_ref[0], slot_ref[...], grad_ref.shape[1])
-    part = dot_dims(dy_ref[...], wide, 1, 1)
+    width, rows = w_ref.shape
+    wide = widen(down_ref[0], slot_ref[...], rows)
+    out = jnp.dot(w_ref[...], wide, preferred_element_type=jnp.float32)
+    rows_ref[0] = (adapter_scale * out).astype(rows_ref.dtype)
+    part = dot_dims(dy_ref[0, :width], wide, 1, 1)
 
     @pl.when(step == 0)
     def _():
@@ -72,23 +84,114 @@
         grad_ref[...] = (adapter_scale * total[...]).astype(grad_ref.dtype)
 
 
-def out_kernel(slot_ref, down_ref, w_ref, base_ref, o_ref):
-    wide = widen(down_ref[...], slot_ref[...], w_ref.shape[0])
-    rows = (adapter_scale * dot_dims(wide, w_ref[...], 0, 0)).astype(jnp.bfloat16)
-    o_ref[...] = (base_ref[...] + rows.astype(jnp.float32)).astype(o_ref.dtype)
+def sum_kernel(n_d, n_t, part_ref, out_ref, from_t, own_t, from_d, own_d, all_d, send, recv):
+    me_d, me_t = lax.axis_index("dp"), lax.axis_index("tensor")
+    peers_d = [lax.rem(me_d + k, n_d) for k in range(n_d)]
+    peers_t = [lax.rem(me_t + k, n_t) for k in range(n_t)]
+
+    barrier = pltpu.get_barrier_semaphore()
+    for peer in peers_t[1:]:
+        pl.semaphore_signal(
+            barrier, inc=1, device_id=(me_d, peer), device_id_type=pl.DeviceIdType.MESH
+        )
+    for peer in peers_d[1:]:
+        pl.semaphore_signal(
+            barrier, inc=1, device_id=(peer, me_t), device_id_type=pl.DeviceIdType.MESH
+        )
+    pl.semaphore_wait(barrier, n_d + n_t - 2)
+
+    base = 0
+
+    def copy(src, dst, device, index):
+        made = pltpu.make_async_remote_copy(
+            src_ref=src,
+            dst_ref=dst,
+            send_sem=send.at[index],
+            recv_sem=recv.at[index],
+            device_id=device,
+            device_id_type=pl.DeviceIdType.MESH,
+        )
+        made.start()
+        return made
+
+    made = [
+        copy(part_ref.at[:, peers_t[k]], from_t.at[k - 1], (me_d, peers_t[k]), base + k - 1)
+        for k in range(1, n_t)
+    ]
+    base += n_t - 1
+    for one in made:
+        one.wait()
+    total = part_ref[:, me_t].astype(jnp.float32)
+    for k in range(n_t - 1):
+        total = total + from_t[k].astype(jnp.float32)
+    own_t[...] = total.astype(own_t.dtype)
+
+    made = [
+        copy(own_t.at[peers_d[k]], from_d.at[k - 1], (peers_d[k], me_t), base + k - 1)
+        for k in range(1, n_d)
+    ]
+    base += n_d - 1
+    for one in made:
+        one.wait()
+    total = own_t[me_d].astype(jnp.float32)
+    for k in range(n_d - 1):
+        total = total + from_d[k].astype(jnp.float32)
+    own_d[...] = total.astype(own_d.dtype)
+
+    made = [
+        copy(own_d, all_d.at[me_d], (peers_d[k], me_t), base + k - 1) for k in range(1, n_d)
+    ]
+    base += n_d - 1
+    all_d[me_d] = own_d[...]
+    for one in made:
+        one.wait()
+
+    made = [
+        copy(all_d, out_ref.at[:, me_t], (me_d, peers_t[k]), base + k - 1)
+        for k in range(1, n_t)
+    ]
+    out_ref[:, me_t] = all_d[...]
+    for one in made:
+        one.wait()
 
 
 def cost(flops, nbytes):
     return pl.CostEstimate(flops=int(flops), bytes_accessed=int(nbytes), transcendentals=0)
 
 
-def project(slots, x, w, rank, tokens, scale, name):
+def sum_all(part):
+    n_d, n_t = lax.axis_size("dp"), lax.axis_size("tensor")
+    _, rank, tokens = part.shape
+    q = rank // n_t
+    vmem = pl.BlockSpec(memory_space=pltpu.VMEM)
+    copies = 2 * (n_d + n_t - 2)
+    return pl.pallas_call(
+        functools.partial(sum_kernel, n_d, n_t),
+        out_shape=jax.ShapeDtypeStruct((n_d, n_t, q, tokens), part.dtype),
+        in_specs=[vmem],
+        out_specs=vmem,
+        scratch_shapes=[
+            pltpu.VMEM((n_t - 1, n_d, q, tokens), part.dtype),
+            pltpu.VMEM((n_d, q, tokens), part.dtype),
+            pltpu.VMEM((n_d - 1, q, tokens), part.dtype),
+            pltpu.VMEM((q, tokens), part.dtype),
+            pltpu.VMEM((n_d, q, tokens), part.dtype),
+            pltpu.SemaphoreType.DMA((copies,)),
+            pltpu.SemaphoreType.DMA((copies,)),
+        ],
+        compiler_params=pltpu.CompilerParams(collective_id=0, has_side_effects=True),
+        cost_estimate=cost(1e9, 4e7),
+        name="sum_all",
+    )(part.reshape(n_d, n_t, q, tokens)).reshape(n_d, rank, tokens)
+
+
+def project_down(slots, x, w, rank, tokens):
     total_tokens, width = x.shape
     rows = w.shape[0]
     blocks = total_tokens // tokens
     return pl.pallas_call(
-        functools.partial(project_kernel, rank, scale),
-        out_shape=jax.ShapeDtypeStruct((blocks, rank, tokens), jnp.float32),
+        functools.partial(down_kernel, rank),
+        out_shape=jax.ShapeDtypeStruct((blocks, rank, tokens), jnp.bfloat16),
         grid=(blocks,),
         in_specs=[
             pl.BlockSpec((1, tokens), lambda i: (0, i)),
@@ -97,8 +200,26 @@
         ],
         out_specs=pl.BlockSpec((1, rank, tokens), lambda i: (i, 0, 0)),
         cost_estimate=cost(2 * total_tokens * rows * width, 2 * (total_tokens + rows) * width),
-        name=name,
+        name="down",
     )(slots, x, w)
+
+
+def project_up(slots, dy, w, rank):
+    blocks, dy_rows, tokens = dy.shape
+    width, rows = w.shape
+    return pl.pallas_call(
+        functools.partial(up_kernel, rank),
+        out_shape=jax.ShapeDtypeStruct((blocks, rank, tokens), jnp.bfloat16),
+        grid=(blocks,),
+        in_specs=[
+            pl.BlockSpec((1, tokens), lambda i: (0, i)),
+            pl.BlockSpec((1, dy_rows, tokens), lambda i: (i, 0, 0)),
+            pl.BlockSpec((width, rows), lambda i: (0, 0)),
+        ],
+        out_specs=pl.BlockSpec((1, rank, tokens), lambda i: (i, 0, 0)),
+        cost_estimate=cost(2 * blocks * tokens * rows * width, 4 * (blocks * tokens + rows) * width),
+        name="up_back",
+    )(slots, dy, w)
 
 
 def back(slots, up_all, x, w, tokens):
@@ -129,34 +250,31 @@
     )(slots, up_all, x, w)
 
 
-def up_grad(slots, down_all, dy, rows, tokens):
-    width, total_tokens = dy.shape
+def up_grad(slots, down_all, dy, w):
+    blocks, dy_rows, tokens = dy.shape
+    width, rows = w.shape
     rank = down_all.shape[1]
-    blocks = total_tokens // tokens
     return pl.pallas_call(
         up_grad_kernel,
-        out_shape=jax.ShapeDtypeStruct((width, rows), jnp.bfloat16),
+        out_shape=(
+            jax.ShapeDtypeStruct((blocks, width, tokens), jnp.bfloat16),
+            jax.ShapeDtypeStruct((width, rows), jnp.bfloat16),
+        ),
         grid=(blocks,),
         in_specs=[
             pl.BlockSpec((1, tokens), lambda i: (0, i)),
             pl.BlockSpec((1, rank, tokens), lambda i: (i, 0, 0)),
-            pl.BlockSpec((width, tokens), lambda i: (0, i)),
-        ],
-        out_specs=pl.BlockSpec((width, rows), lambda i: (0, 0)),
+            pl.BlockSpec((1, dy_rows, tokens), lambda i: (i, 0, 0)),
+            pl.BlockSpec((width, rows), lambda i: (0, 0)),
+        ],
+        out_specs=(
+            pl.BlockSpec((1, width, tokens), lambda i: (i, 0, 0)),
+            pl.BlockSpec((width, rows), lambda i: (0, 0)),
+        ),
         scratch_shapes=[pltpu.VMEM((width, rows), jnp.float32)],
-        cost_estimate=cost(2 * total_tokens * rows * width, 2 * (total_tokens + rows) * width),
+        cost_estimate=cost(4 * blocks * tokens * rows * width, 4 * (blocks * tokens + rows) * width),
         name="up_grad",
-    )(slots, down_all, dy)
-
-
-def add_out(slots, down, w, base):
-    tokens, width = base.shape
-    return pl.pallas_call(
-        out_kernel,
-        out_shape=jax.ShapeDtypeStruct((tokens, width), jnp.bfloat16),
-        cost_estimate=cost(2 * tokens * w.shape[0] * width, 2 * w.shape[0] * width),
-        name="add_out",
-    )(slots, down, w, base)
+    )(slots, down_all, dy, w)
 
 
 def body(
@@ -175,32 +293,41 @@
     down_matrix = adapter_down_weight.reshape(local_count * rank, width_local)
     up_matrix = adapter_up_weight.reshape(local_count * rank, output_local)
 
+    groups = lax.axis_size("dp")
+    part_width = output_local // groups
+
     def exchange(array, split, concat):
         return lax.all_to_all(array, "dp", split_axis=split, concat_axis=concat, tiled=True)
 
-    up_rows = lax.all_gather(up_matrix, "dp", axis=0, tiled=True)
     ids = jnp.arange(all_count, dtype=jnp.int32)
     matches = token_adapter_index[:, None] == ids[None, :]
     slot_tok = jnp.sum(jnp.where(matches, adapter_position[None, :], 0), axis=1)
-    slots = slot_tok.reshape(1, tokens)
-    slots_all = lax.all_gather(slot_tok, "dp", axis=0, tiled=True).reshape(1, -1)
+    digits = jnp.stack([slot_tok // 64, slot_tok % 64]).astype(jnp.bfloat16)
+    pad_rows = (-part_width - 2) % 16
+    tail = jnp.concatenate([digits, jnp.zeros((pad_rows, tokens), jnp.bfloat16)], axis=0)
+    dy_send = jnp.concatenate(
+        [
+            output_gradient.T.reshape(groups, part_width, tokens),
+            jnp.broadcast_to(tail[None], (groups, 2 + pad_rows, tokens)),
+        ],
+        axis=1,
+    )
+    dy_cols = exchange(dy_send, 0, 0)
+    up_cols = exchange(up_matrix.T, 0, 1)
+    got = dy_cols[:, part_width : part_width + 2].astype(jnp.int32)
+    slots_all = (got[:, 0] * 64 + got[:, 1]).reshape(1, groups * tokens)
 
     down_cols = exchange(down_matrix, 1, 0)
     feature_cols = exchange(features, 1, 0)
-    dy_cols = exchange(output_gradient.T, 0, 1)
-
-    up_part = project(slots, output_gradient, up_rows, rank, tokens, adapter_scale, "up_back")
-    up_own = lax.psum(up_part[0], "tensor").astype(jnp.bfloat16)
-    up_all = lax.all_gather(up_own, "dp", axis=0, tiled=False)
-
-    down_part = project(slots_all, feature_cols, down_cols, rank, tokens, 1.0, "down")
-    down_all = lax.psum(down_part, ("dp", "tensor")).astype(jnp.bfloat16)
-
+
+    up_all = sum_all(project_up(slots_all, dy_cols, up_cols, rank))
     in_cols, down_grad_cols = back(slots_all, up_all, feature_cols, down_cols, tokens)
     lora_in = exchange(in_cols, 0, 1)
     down_gradient = exchange(down_grad_cols, 0, 1)
 
-    up_grad_cols = up_grad(slots_all, down_all, dy_cols, all_count * rank, tokens)
+    down_all = sum_all(project_down(slots_all, feature_cols, down_cols, rank, tokens))
+    out_cols, up_grad_cols = up_grad(slots_all, down_all, dy_cols, up_cols)
+    lora_out = exchange(out_cols, 0, 0).reshape(output_local, tokens)
     up_gradient = exchange(up_grad_cols, 1, 0)
 
     gradient_frozen = dot_dims(
@@ -208,9 +335,8 @@
     )
     key_value_frozen = lax.psum_scatter(
         dot_dims(key_value_weight, features, 0, 1), "tensor", scatter_dimension=0, tiled=True
-    ).T
-    down_own = lax.dynamic_index_in_dim(down_all, lax.axis_index("dp"), 0, keepdims=False)
-    key_value_output = add_out(slots, down_own, up_rows, key_value_frozen)
+    )
+    key_value_output = (key_value_frozen + lora_out.astype(jnp.float32)).astype(jnp.bfloat16).T
     feature_gradient = (gradient_frozen + lora_in.astype(jnp.float32)).astype(jnp.bfloat16)
     return (
         key_value_output,

time: 357 us -> 291 us (0.82)
  blocking collectives: 157 us -> 28.9 us
  Pallas kernels: 36.9 us -> 97.5 us
  starting transfers between devices: 29.6 us -> 42.3 us
  waiting for transfers between devices: 76.7 us -> 65.1 us
  other arithmetic: 1.99 us -> 6.18 us
    psum x2 -> x0, blocking collectives: 67.6 us -> none  [the longest x1 54.3 us: body(): down_all = lax.psum(down_part, ('dp', 'tensor')).astype(jnp.bfloat16)]
    all_gather x2 -> x0, blocking collectives: 61.2 us -> none  [the longest x1 37.1 us: body(): lax.all_gather(slot_tok, 'dp', axis=0, tiled=True).reshape(1, -1)]
    pallas_call x4 -> x5, Pallas kernels: 23.4 us -> 83.9 us  [the longest x2 57.8 us: sum_all(): pl.pallas_call(functools.partial(sum_kernel, n_d, n_t), out_shape=jax.Sha...]
    all_to_all x5 -> x7, starting transfers between devices: 29.6 us -> 42.3 us  [exchange(): lax.all_to_all(array, 'dp', split_axis=split, concat_axis=concat, tiled=T...]
    all_to_all x5 -> x7, waiting for transfers between devices: 75.4 us -> 64.4 us  [exchange(): lax.all_to_all(array, 'dp', split_axis=split, concat_axis=concat, tiled=T...]
  transfers between devices with their start and end apart: 8 -> 9, of which waited for: 3 -> 4; matrix products, arithmetic and copies ran while one was open for 7% -> 11% of each run, Pallas kernels for 11% -> 34%
where the time goes in v2:
time: 291 us; the launch traced here: 287 us
  Pallas kernels  97.5 us (34%)
  waiting for transfers between devices  65.1 us (22%)
  starting transfers between devices  42.3 us (15%)
  blocking collectives  28.9 us (10%)
  matrix products  17.1 us (6%)
  local copies, waits for them, and re-layouts  15.4 us (5%)
  between operations  14.2 us (5%)
  other arithmetic  6.18 us (2%)
    all_to_all x7, waiting for transfers between devices, exchange(): lax.all_to_all(array, 'dp', split_axis=split, concat_axis=concat, tiled=T...  64.4 us
    pallas_call x2, Pallas kernels, sum_all(): pl.pallas_call(functools.partial(sum_kernel, n_d, n_t), out_shape=jax.Sha...  57.8 us
    all_to_all x7, starting transfers between devices, exchange(): lax.all_to_all(array, 'dp', split_axis=split, concat_axis=concat, tiled=T...  42.3 us
    all_to_all x1, blocking collectives, exchange(): lax.all_to_all(array, 'dp', split_axis=split, concat_axis=concat, tiled=T...  28.9 us
    dot_general x2, matrix products, dot_dims(): lax.dot_general(left, right, (((left_dim,), (right_dim,)), ((), ())), pre...  17.1 us
    pallas_call x1, Pallas kernels, back(): pl.pallas_call(back_kernel, out_shape=(jax.ShapeDtypeStruct((total_tokens...  13.6 us
    pallas_call x1, Pallas kernels, up_grad(): pl.pallas_call(up_grad_kernel, out_shape=(jax.ShapeDtypeStruct((blocks, w...  10 us
    pallas_call x1, Pallas kernels, project_down(): pl.pallas_call(functools.partial(down_kernel, rank), out_shape=jax.ShapeD...  8.61 us
  transfers between devices with their start and end apart: 9, of which 4 were waited for; matrix products, arithmetic and copies ran while one was open for 11% of the time, Pallas kernels for 34%

profile of v2, /device:TPU:11, one launch (start us, length us, event | category | flops | bytes accessed | tf_op | source)
XLA Modules:
  0.0 286.7 jit_solution(17595944454988700855)
XLA Ops:
  7.2 1.9 copy.40
  9.1 5.7 %all-to-all-start.3 = ((bf16[8,64,256]{2,1,0:T(8,128)(2,1)}), bf16[8,64,256]{2,1,0:T(8,128)(2,1)S(1)}, u32[]{:S(2)}, u32[]{:S(2)}) async-start(bf16[8,64,256]{2,1,0:T(8,128)(2,1)} %bitcast.11), calls=%async_computation.4 | async-start | bytes 524288 | tf_op jit(solution)/shard_map/all_to_all | solution.py:300
  17.6 3.2 %all-to-all-done.3 = bf16[8,64,256]{2,1,0:T(8,128)(2,1)S(1)} async-done(((bf16[8,64,256]{2,1,0:T(8,128)(2,1)}), bf16[8,64,256]{2,1,0:T(8,128)(2,1)S(1)}, u32[]{:S(2)}, u32[]{:S(2)}) %all-to-all-start.3) | async-done | bytes 262176 | tf_op jit(solution)/shard_map/all_to_all | solution.py:300
  20.8 6.1 %all-to-all-start = ((bf16[8,80,384]{2,1,0:T(8,128)(2,1)}), bf16[8,80,384]{2,1,0:T(8,128)(2,1)S(1)}, u32[]{:S(2)}, u32[]{:S(2)}) async-start(bf16[8,80,384]{2,1,0:T(8,128)(2,1)} %pad_maximum_fusion), calls=%async_computation.1 | async-start | bytes 983040 | tf_op jit(solution)/shard_map/all_to_all | solution.py:300
  28.4 9.5 %all-to-all-done.dy_ref = bf16[8,80,384]{2,1,0:T(8,128)(2,1)S(1)} async-done(((bf16[8,80,384]{2,1,0:T(8,128)(2,1)}), bf16[8,80,384]{2,1,0:T(8,128)(2,1)S(1)}, u32[]{:S(2)}, u32[]{:S(2)}) %all-to-all-start) | async-done | bytes 491552 | tf_op jit(solution)/shard_map/all_to_all | solution.py:300
  37.9 6.3 %all-to-all-start.2 = ((bf16[256,8,256]{2,0,1:T(8,128)(2,1)}), bf16[256,8,256]{2,0,1:T(8,128)(2,1)S(1)}, u32[]{:S(2)}, u32[]{:S(2)}) async-start(bf16[256,8,256]{2,0,1:T(8,128)(2,1)} %copy.39), calls=%async_computation.3 | async-start | bytes 2097152 | tf_op jit(solution)/shard_map/all_to_all | solution.py:300
  46.2 21.2 %all-to-all-done.2 = bf16[256,8,256]{2,0,1:T(8,128)(2,1)S(1)} async-done(((bf16[256,8,256]{2,0,1:T(8,128)(2,1)}), bf16[256,8,256]{2,0,1:T(8,128)(2,1)S(1)}, u32[]{:S(2)}, u32[]{:S(2)}) %all-to-all-start.2) | async-done | bytes 1048608 | tf_op jit(solution)/shard_map/all_to_all | solution.py:300
  68.4 6.3 %all-to-all-start.1 = ((bf16[384,8,256]{2,0,1:T(8,128)(2,1)}), bf16[384,8,256]{2,0,1:T(8,128)(2,1)S(1)}, u32[]{:S(2)}, u32[]{:S(2)}) async-start(bf16[384,8,256]{2,0,1:T(8,128)(2,1)} %bitcast.52), calls=%async_computation.2 | async-start | bytes 3145728 | tf_op jit(solution)/shard_map/all_to_all | solution.py:300
  74.7 8.6 %fusion.7 = f32[2048,384]{1,0:T(8,128)} fusion(bf16[2048,2048]{1,0:T(8,128)(2,1)} %param.8, bf16[384,2048]{1,0:T(8,128)(2,1)S(1)} %copy-done), kind=kOutput, calls=%fused_computation.25 | convolution fusion | flops 3221225472 | bytes 13107200 | tf_op jit(solution)/shard_map/dot_general | solution.py:14
  85.6 7.5 %up_back.1 = bf16[8,64,384]{2,1,0:T(8,128)(2,1)} custom-call(s32[1,3072]{1,0:T(1,128)} %bitcast.72, bf16[8,80,384]{2,1,0:T(8,128)(2,1)} %copy-done.4, bf16[64,2048]{1,0:T(8,128)(2,1)} %bitcast.69), custom_call_target="tpu_custom_call" | custom-call | flops 805306368 | bytes 1310720 | tf_op jit(solution)/shard_map/up_back/pallas_call | solution.py:210
  93.1 33.6 %sum_all.3 = bf16[8,4,16,384]{3,2,1,0:T(8,128)(2,1)} custom-call(bf16[8,4,16,384]{3,2,1,0:T(8,128)(2,1)} %bitcast.78), custom_call_target="tpu_custom_call" | custom-call | flops 1000000000 | bytes 40000000 | tf_op jit(solution)/shard_map/sum_all/pallas_call | solution.py:168
  127.8 8.6 %down.1 = bf16[8,64,384]{2,1,0:T(8,128)(2,1)} custom-call(s32[1,3072]{1,0:T(1,128)} %bitcast.73, bf16[3072,256]{1,0:T(8,128)(2,1)} %bitcast.58, bf16[2048,256]{1,0:T(8,128)(2,1)} %bitcast.63), custom_call_target="tpu_custom_call" | custom-call | flops 3221225472 | bytes 2621440 | tf_op jit(solution)/shard_map/down/pallas_call | solution.py:192
  136.4 24.2 %sum_all.2 = bf16[8,4,16,384]{3,2,1,0:T(8,128)(2,1)} custom-call(bf16[8,4,16,384]{3,2,1,0:T(8,128)(2,1)} %bitcast.79), custom_call_target="tpu_custom_call" | custom-call | flops 1000000000 | bytes 40000000 | tf_op jit(solution)/shard_map/sum_all/pallas_call | solution.py:168
  160.6 10.0 %up_grad.1 = (bf16[8,64,384]{2,1,0:T(8,128)(2,1)}, bf16[64,2048]{1,0:T(8,128)(2,1)}) custom-call(s32[1,3072]{1,0:T(1,128)} %bitcast.74, bf16[8,64,384]{2,1,0:T(8,128)(2,1)} %bitcast.77, bf16[8,80,384]{2,1,0:T(8,128)(2,1)} %copy-done.4, bf16[64,2048]{1,0:T(8,128)(2,1)} %bitcast.70), custom_call_target="tpu_custom_call" | custom-call | flops 1610612736 | bytes 1310720 | tf_op jit(solution)/shard_map/up_grad/pallas_call | solution.py:257
  170.7 1.7 copy.55
  172.3 4.6 %all-to-all-start.7 = ((bf16[64,8,256]{2,0,1:T(8,128)(2,1)}), bf16[64,8,256]{2,0,1:T(8,128)(2,1)S(1)}, u32[]{:S(2)}, u32[]{:S(2)}) async-start(bf16[64,8,256]{2,0,1:T(8,128)(2,1)} %bitcast.53), calls=%async_computation.8 | async-start | bytes 524288 | tf_op jit(solution)/shard_map/all_to_all | solution.py:300
  177.0 13.6 %back.1 = (bf16[3072,256]{1,0:T(8,128)(2,1)}, bf16[2048,256]{1,0:T(8,128)(2,1)}) custom-call(s32[1,3072]{1,0:T(1,128)} %bitcast.75, bf16[8,64,384]{2,1,0:T(8,128)(2,1)} %bitcast.76, bf16[3072,256]{1,0:T(8,128)(2,1)} %bitcast.59, bf16[2048,256]{1,0:T(8,128)(2,1)} %bitcast.64), custom_call_target="tpu_custom_call" | custom-call | flops 6442450944 | bytes 5242880 | tf_op jit(solution)/shard_map/back/pallas_call | solution.py:230
  190.5 28.9 %all_to_all.106 = bf16[8,256,256]{2,1,0:T(8,128)(2,1)S(1)} all-to-all(bf16[8,256,256]{2,1,0:T(8,128)(2,1)} %bitcast.65), channel_id=1, replica_groups=mesh['dp'=8,'tensor'=4] {'dp'}, dimensions={0} | all-to-all | bytes 2097152 | tf_op jit(solution)/shard_map/all_to_all | solution.py:300
  219.5 6.7 %all-to-all-start.5 = ((bf16[8,384,256]{2,1,0:T(8,128)(2,1)}), bf16[8,384,256]{2,1,0:T(8,128)(2,1)}, u32[]{:S(2)}, u32[]{:S(2)}) async-start(bf16[8,384,256]{2,1,0:T(8,128)(2,1)} %bitcast.19), calls=%async_computation.6 | async-start | bytes 3145728 | tf_op jit(solution)/shard_map/all_to_all | solution.py:300
  228.7 1.5 reshape.172
  230.2 30.5 %all-to-all-done.5 = bf16[8,384,256]{2,1,0:T(8,128)(2,1)} async-done(((bf16[8,384,256]{2,1,0:T(8,128)(2,1)}), bf16[8,384,256]{2,1,0:T(8,128)(2,1)}, u32[]{:S(2)}, u32[]{:S(2)}) %all-to-all-start.5) | async-done | bytes 1572896 | tf_op jit(solution)/shard_map/all_to_all | solution.py:300
  260.7 6.5 %all-to-all-start.4 = ((bf16[8,64,384]{2,1,0:T(8,128)(2,1)}), bf16[8,64,384]{2,1,0:T(8,128)(2,1)S(1)}, u32[]{:S(2)}, u32[]{:S(2)}) async-start(bf16[8,64,384]{2,1,0:T(8,128)(2,1)} %get-tuple-element.8), calls=%async_computation.5 | async-start | bytes 786432 | tf_op jit(solution)/shard_map/all_to_all | solution.py:300
  267.1 1.7 convert_bitcast_fusion
  269.3 8.5 %add_convert_fusion = bf16[384,2048]{1,0:T(8,128)(2,1)} fusion(f32[384,2048]{1,0:T(8,128)S(1)} %bitcast.55, bf16[384,2048]{1,0:T(8,128)(2,1)} %all-gather.2.cloned.1.call-done, bf16[2048,2048]{1,0:T(8,128)(2,1)} %param.8), kind=kOutput, calls=%fused_computation.1 | convolution fusion | flops 3222798336 | bytes 14680064 | tf_op jit(solution)/shard_map/dot_general | solution.py:14
  (38 shorter events, 15.6 us)
Async XLA Ops:
  7.2 19.7 %copy-start.2 = (bf16[4,64,2048]{2,1,0:T(8,128)(2,1)S(1)}, bf16[4,64,2048]{2,1,0:T(8,128)(2,1)}, u32[]{:S(2)}) copy-start(bf16[4,64,2048]{2,1,0:T(8,128)(2,1)} %param.9) | copy-start | bytes 3145732
  9.1 11.7 %all-to-all-start.3 = ((bf16[8,64,256]{2,1,0:T(8,128)(2,1)}), bf16[8,64,256]{2,1,0:T(8,128)(2,1)S(1)}, u32[]{:S(2)}, u32[]{:S(2)}) async-start(bf16[8,64,256]{2,1,0:T(8,128)(2,1)} %bitcast.11), calls=%async_computation.4 | async-start | bytes 524288 | tf_op jit(solution)/shard_map/all_to_all | solution.py:300
  20.8 17.1 %all-to-all-start = ((bf16[8,80,384]{2,1,0:T(8,128)(2,1)}), bf16[8,80,384]{2,1,0:T(8,128)(2,1)S(1)}, u32[]{:S(2)}, u32[]{:S(2)}) async-start(bf16[8,80,384]{2,1,0:T(8,128)(2,1)} %pad_maximum_fusion), calls=%async_computation.1 | async-start | bytes 983040 | tf_op jit(solution)/shard_map/all_to_all | solution.py:300
  27.2 17.8 %copy-start = (bf16[384,2048]{1,0:T(8,128)(2,1)S(1)}, bf16[384,2048]{1,0:T(8,128)(2,1)}, u32[]{:S(2)}) copy-start(bf16[384,2048]{1,0:T(8,128)(2,1)} %param.7) | copy-start | bytes 4718596
  37.9 8.3 %copy-start.4 = (bf16[8,80,384]{2,1,0:T(8,128)(2,1)}, bf16[8,80,384]{2,1,0:T(8,128)(2,1)S(1)}, u32[]{:S(2)}) copy-start(bf16[8,80,384]{2,1,0:T(8,128)(2,1)S(1)} %all-to-all-done.dy_ref) | copy-start | bytes 1474564
  37.9 29.5 %all-to-all-start.2 = ((bf16[256,8,256]{2,0,1:T(8,128)(2,1)}), bf16[256,8,256]{2,0,1:T(8,128)(2,1)S(1)}, u32[]{:S(2)}, u32[]{:S(2)}) async-start(bf16[256,8,256]{2,0,1:T(8,128)(2,1)} %copy.39), calls=%async_computation.3 | async-start | bytes 2097152 | tf_op jit(solution)/shard_map/all_to_all | solution.py:300
  44.2 225.1 %all-gather.2.cloned.1.call-start = ((), (), s32[]{:S(2)}) async-start(), calls=%async_computation.10 | async-start | bytes 1966080 | tf_op jit(solution)/shard_map/all_gather | solution.py:334
  67.4 1.0 copy-start.3
  68.4 58.3 %all-to-all-start.1 = ((bf16[384,8,256]{2,0,1:T(8,128)(2,1)}), bf16[384,8,256]{2,0,1:T(8,128)(2,1)S(1)}, u32[]{:S(2)}, u32[]{:S(2)}) async-start(bf16[384,8,256]{2,0,1:T(8,128)(2,1)} %bitcast.52), calls=%async_computation.2 | async-start | bytes 3145728 | tf_op jit(solution)/shard_map/all_to_all | solution.py:300
  74.7 203.0 %reduce-scatter.2.cloned.1.call-start = ((), (), s32[]{:S(2)}) async-start(), calls=%async_computation.9 | async-start | bytes 3932160 | tf_op jit(solution)/shard_map/reduce_scatter | solution.py:336
  126.7 1.1 copy-start.1
  172.3 18.2 %all-to-all-start.7 = ((bf16[64,8,256]{2,0,1:T(8,128)(2,1)}), bf16[64,8,256]{2,0,1:T(8,128)(2,1)S(1)}, u32[]{:S(2)}, u32[]{:S(2)}) async-start(bf16[64,8,256]{2,0,1:T(8,128)(2,1)} %bitcast.53), calls=%async_computation.8 | async-start | bytes 524288 | tf_op jit(solution)/shard_map/all_to_all | solution.py:300
  219.5 41.2 %all-to-all-start.5 = ((bf16[8,384,256]{2,1,0:T(8,128)(2,1)}), bf16[8,384,256]{2,1,0:T(8,128)(2,1)}, u32[]{:S(2)}, u32[]{:S(2)}) async-start(bf16[8,384,256]{2,1,0:T(8,128)(2,1)} %bitcast.19), calls=%async_computation.6 | async-start | bytes 3145728 | tf_op jit(solution)/shard_map/all_to_all | solution.py:300
  260.7 17.1 %all-to-all-start.4 = ((bf16[8,64,384]{2,1,0:T(8,128)(2,1)}), bf16[8,64,384]{2,1,0:T(8,128)(2,1)S(1)}, u32[]{:S(2)}, u32[]{:S(2)}) async-start(bf16[8,64,384]{2,1,0:T(8,128)(2,1)} %get-tuple-element.8), calls=%async_computation.5 | async-start | bytes 786432 | tf_op jit(solution)/shard_map/all_to_all | solution.py:300
Sparse Core Ops, SparseCore 0:
  46.6 21.6 all-gather.1
  83.5 40.3 reduce-scatter.1

commit v3 on v2

--- a/solution.py
+++ b/solution.py
@@ -153,6 +153,72 @@
     out_ref[:, me_t] = all_d[...]
     for one in made:
         one.wait()
+
+
+def block_view(ref, form, index, n):
+    if form == "lead":
+        return ref.at[index]
+    width = ref.shape[1] // n
+    return ref.at[:, pl.ds(pl.multiple_of(index * width, width), width)]
+
+
+def exchange_kernel(n, forms, *refs):
+    count = len(forms)
+    sources, targets = refs[:count], refs[count : 2 * count]
+    send, recv, own = refs[2 * count :]
+    me_d, me_t = lax.axis_index("dp"), lax.axis_index("tensor")
+    peers = [lax.rem(me_d + k, n) for k in range(n)]
+    barrier = pltpu.get_barrier_semaphore()
+    for peer in peers[1:]:
+        pl.semaphore_signal(
+            barrier, inc=1, device_id=(peer, me_t), device_id_type=pl.DeviceIdType.MESH
+        )
+    pl.semaphore_wait(barrier, n - 1)
+    made = []
+    for at, (source_form, target_form) in enumerate(forms):
+        for k in range(1, n):
+            made.append(
+                pltpu.make_async_remote_copy(
+                    src_ref=block_view(sources[at], source_form, peers[k], n),
+                    dst_ref=block_view(targets[at], target_form, me_d, n),
+                    send_sem=send.at[at * (n - 1) + k - 1],
+                    recv_sem=recv.at[at * (n - 1) + k - 1],
+                    device_id=(peers[k], me_t),
+                    device_id_type=pl.DeviceIdType.MESH,
+                )
+            )
+            made[-1].start()
+    for at, (source_form, target_form) in enumerate(forms):
+        made.append(
+            pltpu.make_async_copy(
+                block_view(sources[at], source_form, me_d, n),
+                block_view(targets[at], target_form, me_d, n),
+                own.at[at],
+            )
+        )
+        made[-1].start()
+    for one in made:
+        one.wait()
+
+
+def exchange_all(arrays, shapes, forms, collective_id):
+    n = lax.axis_size("dp")
+    vmem = pl.BlockSpec(memory_space=pltpu.VMEM)
+    count = len(arrays)
+    return pl.pallas_call(
+        functools.partial(exchange_kernel, n, forms),
+        out_shape=tuple(jax.ShapeDtypeStruct(shape, jnp.bfloat16) for shape in shapes),
+        in_specs=[vmem] * count,
+        out_specs=(vmem,) * count,
+        scratch_shapes=[
+            pltpu.SemaphoreType.DMA((count * (n - 1),)),
+            pltpu.SemaphoreType.DMA((count * (n - 1),)),
+            pltpu.SemaphoreType.DMA((count,)),
+        ],
+        compiler_params=pltpu.CompilerParams(collective_id=collective_id, has_side_effects=True),
+        cost_estimate=cost(1e9, 1e8),
+        name=f"exchange_{collective_id}",
+    )(*arrays)
 
 
 def cost(flops, nbytes):
@@ -312,23 +378,47 @@
         ],
         axis=1,
     )
-    dy_cols = exchange(dy_send, 0, 0)
-    up_cols = exchange(up_matrix.T, 0, 1)
+    own_rows = local_count * rank
+    all_rows = own_rows * groups
+    in_width = width_local // groups
+    direct = in_width % 128 == 0 and own_rows % 128 == 0 and part_width % 16 == 0
+    if direct:
+        dy_cols, up_cols, down_cols = exchange_all(
+            (dy_send, up_matrix.T.reshape(groups, part_width, own_rows), down_matrix),
+            (dy_send.shape, (part_width, all_rows), (groups, own_rows, in_width)),
+            (("lead", "lead"), ("lead", "col"), ("col", "lead")),
+            1,
+        )
+        down_cols = down_cols.reshape(all_rows, in_width)
+    else:
+        dy_cols = exchange(dy_send, 0, 0)
+        up_cols = exchange(up_matrix.T, 0, 1)
+        down_cols = exchange(down_matrix, 1, 0)
     got = dy_cols[:, part_width : part_width + 2].astype(jnp.int32)
     slots_all = (got[:, 0] * 64 + got[:, 1]).reshape(1, groups * tokens)
 
-    down_cols = exchange(down_matrix, 1, 0)
     feature_cols = exchange(features, 1, 0)
 
     up_all = sum_all(project_up(slots_all, dy_cols, up_cols, rank))
     in_cols, down_grad_cols = back(slots_all, up_all, feature_cols, down_cols, tokens)
+    in_cols, slots_late = lax.optimization_barrier((in_cols, slots_all))
     lora_in = exchange(in_cols, 0, 1)
-    down_gradient = exchange(down_grad_cols, 0, 1)
-
-    down_all = sum_all(project_down(slots_all, feature_cols, down_cols, rank, tokens))
+
+    down_all = sum_all(project_down(slots_late, feature_cols, down_cols, rank, tokens))
     out_cols, up_grad_cols = up_grad(slots_all, down_all, dy_cols, up_cols)
-    lora_out = exchange(out_cols, 0, 0).reshape(output_local, tokens)
-    up_gradient = exchange(up_grad_cols, 1, 0)
+    if direct:
+        lora_out, up_gradient, down_gradient = exchange_all(
+            (out_cols, up_grad_cols, down_grad_cols.reshape(groups, own_rows, in_width)),
+            (out_cols.shape, (groups, part_width, own_rows), (own_rows, width_local)),
+            (("lead", "lead"), ("col", "lead"), ("lead", "col")),
+            2,
+        )
+        up_gradient = up_gradient.reshape(output_local, own_rows)
+    else:
+        lora_out = exchange(out_cols, 0, 0)
+        up_gradient = exchange(up_grad_cols, 1, 0)
+        down_gradient = exchange(down_grad_cols, 0, 1)
+    lora_out = lora_out.reshape(output_local, tokens)
 
     gradient_frozen = dot_dims(
         lax.all_gather(output_gradient, "tensor", axis=1, tiled=True), key_value_weight, 1, 1

time: 291 us -> 272 us (0.935); the launches traced: 287 us -> 271 us
  Pallas kernels: 97.5 us -> 213 us
  waiting for transfers between devices: 65.1 us -> 0.73 us
  starting transfers between devices: 42.3 us -> 11 us
  blocking collectives: 28.9 us -> 0 us
  local copies, waits for them, and re-layouts: 15.4 us -> 8.2 us
    pallas_call x0 -> x2, Pallas kernels: none -> 108 us  [exchange_all(): pl.pallas_call(functools.partial(exchange_kernel, n, forms), out_shape=tu...]
    all_to_all x7 -> x2, waiting for transfers between devices: 64.4 us -> 0.01 us  [exchange(): lax.all_to_all(array, 'dp', split_axis=split, concat_axis=concat, tiled=T...]
    all_to_all x7 -> x2, starting transfers between devices: 42.3 us -> 11 us  [exchange(): lax.all_to_all(array, 'dp', split_axis=split, concat_axis=concat, tiled=T...]
    all_to_all x1 -> x0, blocking collectives: 28.9 us -> none  [exchange(): lax.all_to_all(array, 'dp', split_axis=split, concat_axis=concat, tiled=T...]
    pallas_call x2, Pallas kernels: 57.8 us -> 65.9 us  [sum_all(): pl.pallas_call(functools.partial(sum_kernel, n_d, n_t), out_shape=jax.Sha...]
  transfers between devices with their start and end apart: 9 -> 4, of which waited for: 4 -> 0; matrix products, arithmetic and copies ran while one was open for 11% -> 10% of each run, Pallas kernels for 34% -> 79%
where the time goes in v3:
time: 272 us; the launch traced here: 271 us
  Pallas kernels  213 us (78%)
  matrix products  17.3 us (6%)
  between operations  14.2 us (5%)
  starting transfers between devices  11 us (4%)
  local copies, waits for them, and re-layouts  8.2 us (3%)
  other arithmetic  6.74 us (2%)
    pallas_call x2, Pallas kernels, exchange_all(): pl.pallas_call(functools.partial(exchange_kernel, n, forms), out_shape=tu...  108 us
    pallas_call x2, Pallas kernels, sum_all(): pl.pallas_call(functools.partial(sum_kernel, n_d, n_t), out_shape=jax.Sha...  65.9 us
    dot_general x2, matrix products, dot_dims(): lax.dot_general(left, right, (((left_dim,), (right_dim,)), ((), ())), pre...  17.3 us
    pallas_call x1, Pallas kernels, back(): pl.pallas_call(back_kernel, out_shape=(jax.ShapeDtypeStruct((total_tokens...  13.5 us
    all_to_all x2, starting transfers between devices, exchange(): lax.all_to_all(array, 'dp', split_axis=split, concat_axis=concat, tiled=T...  11 us
    pallas_call x1, Pallas kernels, up_grad(): pl.pallas_call(up_grad_kernel, out_shape=(jax.ShapeDtypeStruct((blocks, w...  9.97 us
    pallas_call x1, Pallas kernels, project_down(): pl.pallas_call(functools.partial(down_kernel, rank), out_shape=jax.ShapeD...  8.61 us
    pallas_call x1, Pallas kernels, project_up(): pl.pallas_call(functools.partial(up_kernel, rank), out_shape=jax.ShapeDty...  7.48 us
  transfers between devices with their start and end apart: 4, of which 0 were waited for; matrix products, arithmetic and copies ran while one was open for 10% of the time, Pallas kernels for 79%

profile of v3, /device:TPU:11, one launch (start us, length us, event | category | flops | bytes accessed | tf_op | source)
XLA Modules:
  0.0 271.3 jit_solution(3070483805001789968)
XLA Ops:
  7.2 0.7 all-gather.2.cloned.1.call-update
  7.9 2.7 copy.26
  10.6 5.8 %all-to-all-start = ((bf16[384,8,256]{2,0,1:T(8,128)(2,1)}), bf16[384,8,256]{2,0,1:T(8,128)(2,1)S(1)}, u32[]{:S(2)}, u32[]{:S(2)}) async-start(bf16[384,8,256]{2,0,1:T(8,128)(2,1)} %bitcast.42), calls=%async_computation.1 | async-start | bytes 3145728 | tf_op jit(solution)/shard_map/all_to_all | solution.py:366
  16.4 8.9 %fusion.7 = f32[2048,384]{1,0:T(8,128)} fusion(bf16[2048,2048]{1,0:T(8,128)(2,1)} %param.8, bf16[384,2048]{1,0:T(8,128)(2,1)S(1)} %copy-done), kind=kOutput, calls=%fused_computation.24 | convolution fusion | flops 3221225472 | bytes 13107200 | tf_op jit(solution)/shard_map/dot_general | solution.py:14
  25.3 1.0 copy-done.2
  26.4 0.8 copy.18
  27.4 0.8 pad_maximum_fusion.refs_0_
  28.3 63.7 %exchange_1.1 = (bf16[8,80,384]{2,1,0:T(8,128)(2,1)}, bf16[64,2048]{1,0:T(8,128)(2,1)}, bf16[8,256,256]{2,1,0:T(8,128)(2,1)}) custom-call(bf16[8,80,384]{2,1,0:T(8,128)(2,1)} %pad_maximum_fusion.refs_0_, bf16[8,64,256]{2,1,0:T(8,128)(2,1)} %bitcast.53, bf16[256,2048]{1,0:T(8,128)(2,1)} %bitcast.58), custom_call_target="tpu_custom_call" | custom-call | flops 1000000000 | bytes 100000000 | tf_op jit(solution)/shard_map/exchange_1/pallas_call | solution.py:208
  92.0 0.8 slice_convert_fusion
  92.8 0.6 slice_add_fusion
  93.4 7.5 %up_back.1 = bf16[8,64,384]{2,1,0:T(8,128)(2,1)} custom-call(s32[1,3072]{1,0:T(1,128)} %bitcast.54, bf16[8,80,384]{2,1,0:T(8,128)(2,1)} %get-tuple-element.16.dy_ref, bf16[64,2048]{1,0:T(8,128)(2,1)} %get-tuple-element.17.w_ref), custom_call_target="tpu_custom_call" | custom-call | flops 805306368 | bytes 1310720 | tf_op jit(solution)/shard_map/up_back/pallas_call | solution.py:276
  100.9 25.2 %sum_all.2 = bf16[8,4,16,384]{3,2,1,0:T(8,128)(2,1)} custom-call(bf16[8,4,16,384]{3,2,1,0:T(8,128)(2,1)} %bitcast.65), custom_call_target="tpu_custom_call" | custom-call | flops 1000000000 | bytes 40000000 | tf_op jit(solution)/shard_map/sum_all/pallas_call | solution.py:234
  126.2 1.1 copy-done.1
  127.3 13.5 %back.1 = (bf16[3072,256]{1,0:T(8,128)(2,1)}, bf16[2048,256]{1,0:T(8,128)(2,1)}) custom-call(s32[1,3072]{1,0:T(1,128)} %bitcast.55, bf16[8,64,384]{2,1,0:T(8,128)(2,1)} %bitcast.62, bf16[3072,256]{1,0:T(8,128)(2,1)} %bitcast.45, bf16[2048,256]{1,0:T(8,128)(2,1)} %bitcast.59), custom_call_target="tpu_custom_call" | custom-call | flops 6442450944 | bytes 5242880 | tf_op jit(solution)/shard_map/back/pallas_call | solution.py:296
  140.8 5.2 %all-to-all-start.1 = ((bf16[8,384,256]{2,1,0:T(8,128)(2,1)}), bf16[8,384,256]{2,1,0:T(8,128)(2,1)S(1)}, u32[]{:S(2)}, u32[]{:S(2)}) async-start(bf16[8,384,256]{2,1,0:T(8,128)(2,1)} %bitcast.47), calls=%async_computation.2 | async-start | bytes 3145728 | tf_op jit(solution)/shard_map/all_to_all | solution.py:366
  146.0 8.6 %down.1 = bf16[8,64,384]{2,1,0:T(8,128)(2,1)} custom-call(s32[1,3072]{1,0:T(1,128)} %bitcast.56, bf16[3072,256]{1,0:T(8,128)(2,1)} %bitcast.46, bf16[2048,256]{1,0:T(8,128)(2,1)} %bitcast.60), custom_call_target="tpu_custom_call" | custom-call | flops 3221225472 | bytes 2621440 | tf_op jit(solution)/shard_map/down/pallas_call | solution.py:258
  154.6 40.6 %sum_all.3 = bf16[8,4,16,384]{3,2,1,0:T(8,128)(2,1)} custom-call(bf16[8,4,16,384]{3,2,1,0:T(8,128)(2,1)} %bitcast.64), custom_call_target="tpu_custom_call" | custom-call | flops 1000000000 | bytes 40000000 | tf_op jit(solution)/shard_map/sum_all/pallas_call | solution.py:234
  195.2 10.0 %up_grad.1 = (bf16[8,64,384]{2,1,0:T(8,128)(2,1)}, bf16[64,2048]{1,0:T(8,128)(2,1)}) custom-call(s32[1,3072]{1,0:T(1,128)} %bitcast.57, bf16[8,64,384]{2,1,0:T(8,128)(2,1)} %bitcast.63, bf16[8,80,384]{2,1,0:T(8,128)(2,1)} %get-tuple-element.16.dy_ref, bf16[64,2048]{1,0:T(8,128)(2,1)} %get-tuple-element.17.w_ref), custom_call_target="tpu_custom_call" | custom-call | flops 1610612736 | bytes 1310720 | tf_op jit(solution)/shard_map/up_grad/pallas_call | solution.py:323
  205.2 43.9 %exchange_2.1 = (bf16[8,64,384]{2,1,0:T(8,128)(2,1)}, bf16[8,64,256]{2,1,0:T(8,128)(2,1)}, bf16[256,2048]{1,0:T(8,128)(2,1)}) custom-call(bf16[8,64,384]{2,1,0:T(8,128)(2,1)} %get-tuple-element.21.refs_0_, bf16[64,2048]{1,0:T(8,128)(2,1)} %get-tuple-element.22.refs_1_, bf16[8,256,256]{2,1,0:T(8,128)(2,1)} %bitcast.61), custom_call_target="tpu_custom_call" | custom-call | flops 1000000000 | bytes 100000000 | tf_op jit(solution)/shard_map/exchange_2/pallas_call | solution.py:208
  249.1 2.8 %convert.16 = f32[4,64,2048]{2,1,0:T(8,128)} convert(bf16[4,64,2048]{2,1,0:T(8,128)(2,1)} %bitcast.50) | non-fusion elementwise | flops 524288 | bytes 3145728 | tf_op jit(solution)/shard_map/reshape | solution.py:434
  252.0 1.0 copy.21
  253.8 8.5 %add_convert_fusion = bf16[384,2048]{1,0:T(8,128)(2,1)} fusion(f32[384,2048]{1,0:T(8,128)S(1)} %bitcast.43, bf16[384,2048]{1,0:T(8,128)(2,1)} %all-gather.2.cloned.1.call-done, bf16[2048,2048]{1,0:T(8,128)(2,1)} %param.8), kind=kOutput, calls=%fused_computation.1 | convolution fusion | flops 3222798336 | bytes 14680064 | tf_op jit(solution)/shard_map/dot_general | solution.py:14
  262.3 1.2 fusion.1
  263.5 0.9 copy.22
  (29 shorter events, 1.2 us)
Async XLA Ops:
  7.2 246.6 %all-gather.2.cloned.1.call-start = ((), (), s32[]{:S(2)}) async-start(), calls=%async_computation.4 | async-start | bytes 1966080 | tf_op jit(solution)/shard_map/all_gather | solution.py:424
  10.6 5.8 %copy-start = (bf16[384,2048]{1,0:T(8,128)(2,1)S(1)}, bf16[384,2048]{1,0:T(8,128)(2,1)}, u32[]{:S(2)}) copy-start(bf16[384,2048]{1,0:T(8,128)(2,1)} %param.7) | copy-start | bytes 4718596
  10.6 115.6 %all-to-all-start = ((bf16[384,8,256]{2,0,1:T(8,128)(2,1)}), bf16[384,8,256]{2,0,1:T(8,128)(2,1)S(1)}, u32[]{:S(2)}, u32[]{:S(2)}) async-start(bf16[384,8,256]{2,0,1:T(8,128)(2,1)} %bitcast.42), calls=%async_computation.1 | async-start | bytes 3145728 | tf_op jit(solution)/shard_map/all_to_all | solution.py:366
  16.3 245.9 %reduce-scatter.2.cloned.1.call-start = ((), (), s32[]{:S(2)}) async-start(), calls=%async_computation.3 | async-start | bytes 3932160 | tf_op jit(solution)/shard_map/reduce_scatter | solution.py:426
  25.2 1.0 copy-start.2
  25.2 1.2 copy-start.5
  25.2 2.1 copy-start.6
  25.2 2.1 copy-start.7
  126.1 1.1 copy-start.1
  140.8 112.2 %all-to-all-start.1 = ((bf16[8,384,256]{2,1,0:T(8,128)(2,1)}), bf16[8,384,256]{2,1,0:T(8,128)(2,1)S(1)}, u32[]{:S(2)}, u32[]{:S(2)}) async-start(bf16[8,384,256]{2,1,0:T(8,128)(2,1)} %bitcast.47), calls=%async_computation.2 | async-start | bytes 3145728 | tf_op jit(solution)/shard_map/all_to_all | solution.py:366
  249.1 2.8 %copy-start.4 = (bf16[8,64,256]{2,1,0:T(8,128)(2,1)S(1)}, bf16[8,64,256]{2,1,0:T(8,128)(2,1)}, u32[]{:S(2)}) copy-start(bf16[8,64,256]{2,1,0:T(8,128)(2,1)} %get-tuple-element.27) | copy-start | bytes 786436
  253.8 8.5 %copy-start.3 = (bf16[8,64,384]{2,1,0:T(8,128)(2,1)S(1)}, bf16[8,64,384]{2,1,0:T(8,128)(2,1)}, u32[]{:S(2)}) copy-start(bf16[8,64,384]{2,1,0:T(8,128)(2,1)} %get-tuple-element.24) | copy-start | bytes 1179652
Sparse Core Ops, SparseCore 0:
  9.5 21.1 all-gather.1
  33.3 37.3 reduce-scatter.1

commit v4 on v3

--- a/solution.py
+++ b/solution.py
@@ -397,7 +397,8 @@
     got = dy_cols[:, part_width : part_width + 2].astype(jnp.int32)
     slots_all = (got[:, 0] * 64 + got[:, 1]).reshape(1, groups * tokens)
 
-    feature_cols = exchange(features, 1, 0)
+    late, slots_all = lax.optimization_barrier((features, slots_all))
+    feature_cols = exchange(late, 1, 0)
 
     up_all = sum_all(project_up(slots_all, dy_cols, up_cols, rank))
     in_cols, down_grad_cols = back(slots_all, up_all, feature_cols, down_cols, tokens)

time: 272 us -> 265 us (0.974)
  Pallas kernels: 213 us -> 207 us
    pallas_call x2, Pallas kernels: 108 us -> 90.1 us  [exchange_all(): pl.pallas_call(functools.partial(exchange_kernel, n, forms), out_shape=tu...]
    pallas_call x2, Pallas kernels: 65.9 us -> 77 us  [sum_all(): pl.pallas_call(functools.partial(sum_kernel, n_d, n_t), out_shape=jax.Sha...]
  transfers between devices with their start and end apart: 4 -> 4, of which waited for: 0 -> 0; matrix products, arithmetic and copies ran while one was open for 10% -> 11% of each run, Pallas kernels for 79% -> 78%
where the time goes in v4:
time: 265 us; the launch traced here: 264 us
  Pallas kernels  207 us (78%)
  matrix products  17.1 us (6%)
  between operations  14.2 us (5%)
  starting transfers between devices  10.1 us (4%)
  local copies, waits for them, and re-layouts  7.77 us (3%)
  other arithmetic  7.44 us (3%)
    pallas_call x2, Pallas kernels, exchange_all(): pl.pallas_call(functools.partial(exchange_kernel, n, forms), out_shape=tu...  90.1 us
    pallas_call x2, Pallas kernels, sum_all(): pl.pallas_call(functools.partial(sum_kernel, n_d, n_t), out_shape=jax.Sha...  77 us
    dot_general x2, matrix products, dot_dims(): lax.dot_general(left, right, (((left_dim,), (right_dim,)), ((), ())), pre...  17.1 us
    pallas_call x1, Pallas kernels, back(): pl.pallas_call(back_kernel, out_shape=(jax.ShapeDtypeStruct((total_tokens...  13.5 us
    all_to_all x2, starting transfers between devices, exchange(): lax.all_to_all(array, 'dp', split_axis=split, concat_axis=concat, tiled=T...  10 us
    pallas_call x1, Pallas kernels, up_grad(): pl.pallas_call(up_grad_kernel, out_shape=(jax.ShapeDtypeStruct((blocks, w...  10 us
    pallas_call x1, Pallas kernels, project_down(): pl.pallas_call(functools.partial(down_kernel, rank), out_shape=jax.ShapeD...  8.61 us
    pallas_call x1, Pallas kernels, project_up(): pl.pallas_call(functools.partial(up_kernel, rank), out_shape=jax.ShapeDty...  7.52 us
  transfers between devices with their start and end apart: 4, of which 0 were waited for; matrix products, arithmetic and copies ran while one was open for 11% of the time, Pallas kernels for 78%

profile of v4, /device:TPU:11, one launch (start us, length us, event | category | flops | bytes accessed | tf_op | source)
XLA Modules:
  0.0 264.0 jit_solution(8382569685118776180)
XLA Ops:
  7.2 0.7 all-gather.2.cloned.1.call-update
  7.9 1.2 copy.17
  9.1 1.8 copy.18
  10.9 0.8 select_reduce_fusion
  11.8 0.8 pad_maximum_fusion.refs_0_
  12.6 46.5 %exchange_1.1 = (bf16[8,80,384]{2,1,0:T(8,128)(2,1)}, bf16[64,2048]{1,0:T(8,128)(2,1)}, bf16[8,256,256]{2,1,0:T(8,128)(2,1)}) custom-call(bf16[8,80,384]{2,1,0:T(8,128)(2,1)} %pad_maximum_fusion.refs_0_, bf16[8,64,256]{2,1,0:T(8,128)(2,1)} %bitcast.53, bf16[256,2048]{1,0:T(8,128)(2,1)} %bitcast.58), custom_call_target="tpu_custom_call" | custom-call | flops 1000000000 | bytes 100000000 | tf_op jit(solution)/shard_map/exchange_1/pallas_call | solution.py:208
  59.1 0.8 slice_convert_fusion
  60.5 1.2 copy.26
  61.8 4.4 %all-to-all-start = ((bf16[384,8,256]{2,0,1:T(8,128)(2,1)}), bf16[384,8,256]{2,0,1:T(8,128)(2,1)S(1)}, u32[]{:S(2)}, u32[]{:S(2)}) async-start(bf16[384,8,256]{2,0,1:T(8,128)(2,1)} %bitcast.42), calls=%async_computation.1 | async-start | bytes 3145728 | tf_op jit(solution)/shard_map/all_to_all | solution.py:366
  66.2 8.6 %fusion.7 = f32[2048,384]{1,0:T(8,128)} fusion(bf16[2048,2048]{1,0:T(8,128)(2,1)} %param.8, bf16[384,2048]{1,0:T(8,128)(2,1)S(1)} %copy-done), kind=kOutput, calls=%fused_computation.24 | convolution fusion | flops 3221225472 | bytes 13107200 | tf_op jit(solution)/shard_map/dot_general | solution.py:14
  74.8 7.5 %up_back.1 = bf16[8,64,384]{2,1,0:T(8,128)(2,1)} custom-call(s32[1,3072]{1,0:T(1,128)} %bitcast.54, bf16[8,80,384]{2,1,0:T(8,128)(2,1)} %get-tuple-element.18.dy_ref, bf16[64,2048]{1,0:T(8,128)(2,1)} %get-tuple-element.20.w_ref), custom_call_target="tpu_custom_call" | custom-call | flops 805306368 | bytes 1310720 | tf_op jit(solution)/shard_map/up_back/pallas_call | solution.py:276
  82.3 36.8 %sum_all.2 = bf16[8,4,16,384]{3,2,1,0:T(8,128)(2,1)} custom-call(bf16[8,4,16,384]{3,2,1,0:T(8,128)(2,1)} %bitcast.65), custom_call_target="tpu_custom_call" | custom-call | flops 1000000000 | bytes 40000000 | tf_op jit(solution)/shard_map/sum_all/pallas_call | solution.py:234
  119.2 1.1 copy-done.1
  120.3 13.5 %back.1 = (bf16[3072,256]{1,0:T(8,128)(2,1)}, bf16[2048,256]{1,0:T(8,128)(2,1)}) custom-call(s32[1,3072]{1,0:T(1,128)} %bitcast.55, bf16[8,64,384]{2,1,0:T(8,128)(2,1)} %bitcast.62, bf16[3072,256]{1,0:T(8,128)(2,1)} %bitcast.45, bf16[2048,256]{1,0:T(8,128)(2,1)} %bitcast.59), custom_call_target="tpu_custom_call" | custom-call | flops 6442450944 | bytes 5242880 | tf_op jit(solution)/shard_map/back/pallas_call | solution.py:296
  133.9 5.6 %all-to-all-start.1 = ((bf16[8,384,256]{2,1,0:T(8,128)(2,1)}), bf16[8,384,256]{2,1,0:T(8,128)(2,1)S(1)}, u32[]{:S(2)}, u32[]{:S(2)}) async-start(bf16[8,384,256]{2,1,0:T(8,128)(2,1)} %bitcast.47), calls=%async_computation.2 | async-start | bytes 3145728 | tf_op jit(solution)/shard_map/all_to_all | solution.py:366
  139.5 8.6 %down.1 = bf16[8,64,384]{2,1,0:T(8,128)(2,1)} custom-call(s32[1,3072]{1,0:T(1,128)} %bitcast.56, bf16[3072,256]{1,0:T(8,128)(2,1)} %bitcast.46, bf16[2048,256]{1,0:T(8,128)(2,1)} %bitcast.60), custom_call_target="tpu_custom_call" | custom-call | flops 3221225472 | bytes 2621440 | tf_op jit(solution)/shard_map/down/pallas_call | solution.py:258
  148.1 40.1 %sum_all.3 = bf16[8,4,16,384]{3,2,1,0:T(8,128)(2,1)} custom-call(bf16[8,4,16,384]{3,2,1,0:T(8,128)(2,1)} %bitcast.64), custom_call_target="tpu_custom_call" | custom-call | flops 1000000000 | bytes 40000000 | tf_op jit(solution)/shard_map/sum_all/pallas_call | solution.py:234
  188.2 10.0 %up_grad.1 = (bf16[8,64,384]{2,1,0:T(8,128)(2,1)}, bf16[64,2048]{1,0:T(8,128)(2,1)}) custom-call(s32[1,3072]{1,0:T(1,128)} %bitcast.57, bf16[8,64,384]{2,1,0:T(8,128)(2,1)} %bitcast.63, bf16[8,80,384]{2,1,0:T(8,128)(2,1)} %get-tuple-element.18.dy_ref, bf16[64,2048]{1,0:T(8,128)(2,1)} %get-tuple-element.20.w_ref), custom_call_target="tpu_custom_call" | custom-call | flops 1610612736 | bytes 1310720 | tf_op jit(solution)/shard_map/up_grad/pallas_call | solution.py:323
  198.2 43.6 %exchange_2.1 = (bf16[8,64,384]{2,1,0:T(8,128)(2,1)}, bf16[8,64,256]{2,1,0:T(8,128)(2,1)}, bf16[256,2048]{1,0:T(8,128)(2,1)}) custom-call(bf16[8,64,384]{2,1,0:T(8,128)(2,1)} %get-tuple-element.25.refs_0_, bf16[64,2048]{1,0:T(8,128)(2,1)} %get-tuple-element.26.refs_1_, bf16[8,256,256]{2,1,0:T(8,128)(2,1)} %bitcast.61), custom_call_target="tpu_custom_call" | custom-call | flops 1000000000 | bytes 100000000 | tf_op jit(solution)/shard_map/exchange_2/pallas_call | solution.py:208
  241.8 2.8 %convert.16 = f32[4,64,2048]{2,1,0:T(8,128)} convert(bf16[4,64,2048]{2,1,0:T(8,128)(2,1)} %bitcast.50) | non-fusion elementwise | flops 524288 | bytes 3145728 | tf_op jit(solution)/shard_map/reshape | solution.py:435
  244.7 1.0 copy.21
  246.5 8.5 %add_convert_fusion = bf16[384,2048]{1,0:T(8,128)(2,1)} fusion(f32[384,2048]{1,0:T(8,128)S(1)} %bitcast.43, bf16[384,2048]{1,0:T(8,128)(2,1)} %all-gather.2.cloned.1.call-done, bf16[2048,2048]{1,0:T(8,128)(2,1)} %param.8), kind=kOutput, calls=%fused_computation.1 | convolution fusion | flops 3222798336 | bytes 14680064 | tf_op jit(solution)/shard_map/dot_general | solution.py:14
  255.0 1.2 fusion.1
  256.2 0.9 copy.22
  (21 shorter events, 1.5 us)
Async XLA Ops:
  7.2 239.3 %all-gather.2.cloned.1.call-start = ((), (), s32[]{:S(2)}) async-start(), calls=%async_computation.4 | async-start | bytes 1966080 | tf_op jit(solution)/shard_map/all_gather | solution.py:425
  12.6 47.9 %copy-start = (bf16[384,2048]{1,0:T(8,128)(2,1)S(1)}, bf16[384,2048]{1,0:T(8,128)(2,1)}, u32[]{:S(2)}) copy-start(bf16[384,2048]{1,0:T(8,128)(2,1)} %param.7) | copy-start | bytes 4718596
  61.8 57.4 %all-to-all-start = ((bf16[384,8,256]{2,0,1:T(8,128)(2,1)}), bf16[384,8,256]{2,0,1:T(8,128)(2,1)S(1)}, u32[]{:S(2)}, u32[]{:S(2)}) async-start(bf16[384,8,256]{2,0,1:T(8,128)(2,1)} %bitcast.42), calls=%async_computation.1 | async-start | bytes 3145728 | tf_op jit(solution)/shard_map/all_to_all | solution.py:366
  66.2 188.8 %reduce-scatter.2.cloned.1.call-start = ((), (), s32[]{:S(2)}) async-start(), calls=%async_computation.3 | async-start | bytes 3932160 | tf_op jit(solution)/shard_map/reduce_scatter | solution.py:427
  119.2 1.1 copy-start.1
  133.9 111.9 %all-to-all-start.1 = ((bf16[8,384,256]{2,1,0:T(8,128)(2,1)}), bf16[8,384,256]{2,1,0:T(8,128)(2,1)S(1)}, u32[]{:S(2)}, u32[]{:S(2)}) async-start(bf16[8,384,256]{2,1,0:T(8,128)(2,1)} %bitcast.47), calls=%async_computation.2 | async-start | bytes 3145728 | tf_op jit(solution)/shard_map/all_to_all | solution.py:366
  241.8 2.8 %copy-start.3 = (bf16[8,64,256]{2,1,0:T(8,128)(2,1)S(1)}, bf16[8,64,256]{2,1,0:T(8,128)(2,1)}, u32[]{:S(2)}) copy-start(bf16[8,64,256]{2,1,0:T(8,128)(2,1)} %get-tuple-element.31) | copy-start | bytes 786436
  246.5 8.5 %copy-start.2 = (bf16[8,64,384]{2,1,0:T(8,128)(2,1)S(1)}, bf16[8,64,384]{2,1,0:T(8,128)(2,1)}, u32[]{:S(2)}) copy-start(bf16[8,64,384]{2,1,0:T(8,128)(2,1)} %get-tuple-element.28) | copy-start | bytes 1179652
Sparse Core Ops, SparseCore 0:
  9.5 21.1 all-gather.1
  74.9 42.7 reduce-scatter.1
